TPU v7x, 256 devices: a whole 4x4x8 slice. The times are simulated.
256 devices in a mesh: pipe: 2 (over z_lo), ctx: 64 (over z_hi, x, y), tp: 2 (over core).
Axes of the slice: x: 4, y: 4, z: 8 (z_hi: 4, z_lo: 2; z = z_hi * 2 + z_lo), core: 2. Of those that a mesh axis runs over, the one named last changes fastest.
Arguments:
- lin_query: bfloat16 [9216, 4096], P('ctx', 'tp'), may hold values from -6 to 6
- lin_key: bfloat16 [9216, 4096], P('ctx', 'tp'), may hold values from -6 to 6
- lin_value: bfloat16 [9216, 4096], P('ctx', 'tp'), may hold values from -128 to 128
- log_decay: float32 [32, 9216], P('tp', 'ctx'), may hold values from -1 to 0
- out_gate: bfloat16 [9216, 4096], P('ctx', 'tp'), may hold values from -6 to 6
- norm_gain: float32 [4096], P('tp'), may hold values from 0.1 to 1.9
- value_proj: bfloat16 [4, 1024, 128], P('tp'), may hold values from -0.1875 to 0.1875
- soft_query: bfloat16 [9216, 4096], P('ctx', 'tp'), may hold values from -16 to 16
- soft_key: bfloat16 [9216, 512], P('ctx', 'tp'), may hold values from -16 to 16
- doc_lengths: int32 [8], replicated, may hold values from 1 to 6912, 9216 in all
Outputs:
- section_out: bfloat16 [2, 9216, 4096], P('pipe', 'ctx', 'tp')
Inputs may be any that keep to these rules, and one draw needn't show every extreme that they name: `doc_lengths`: they sum to 9216.
All inputs are finite; a program needn't handle non-finite values.
Results may differ from a plain program's by a relative error of at most 0.0028.
The roundings to bfloat16 on the way count: a program that leaves them out, or rounds other values in their place, can miss the bound.
Values may be sent and summed in bfloat16 or wider, within the bound.
A program may use at most 192 MiB of HBM per device.

v0:
```python
import math

import jax
import jax.numpy as jnp
from jax import lax
from jax.sharding import PartitionSpec as P

HEADS = 32
HEAD_DIM = 128


norm_epsilon = 1e-06


def entering(part, axis, combine, identity):
    place = lax.axis_index(axis)
    gathered = jax.tree.map(lambda a: lax.all_gather(a, axis), part)
    state = jax.tree.map(lambda a, e: jnp.zeros_like(a) + jnp.asarray(e, a.dtype), part, identity)

    def one(step, state):
        return combine(
            state, jax.tree.map(lambda a: lax.dynamic_index_in_dim(a, step, 0, False), gathered)
        )

    return lax.fori_loop(0, place, one, state)


def shifted(shard, axis, by):
    devices = lax.axis_size(axis)
    pairs = [(i, i + by) for i in range(devices) if 0 <= i + by < devices]
    return lax.ppermute(shard, axis, pairs)


def doc_numbers(doc_lengths, token_positions):
    doc_ends = jnp.cumsum(doc_lengths)
    return jnp.sum((doc_ends[None, :] <= token_positions[:, None]).astype(jnp.int32), axis=1)


def chain_combine(earlier, later):
    return (earlier[0] * later[0], later[0][:, None, None] * earlier[1] + later[1])


def lightning_section(lin_query, lin_key, lin_value, log_decay, out_gate, norm_gain, doc_lengths):
    row_count, features = lin_query.shape
    head_count = log_decay.shape[0]
    head_size = features // head_count
    first_pos = lax.axis_index("ctx") * row_count
    token_positions = first_pos + jnp.arange(row_count, dtype=jnp.int32)
    doc_ids = doc_numbers(doc_lengths, token_positions)
    before_doc = doc_numbers(doc_lengths, jnp.reshape(first_pos - 1, (1,)))[0]
    prev_doc = jnp.where(first_pos > 0, before_doc, -1)
    queries = lin_query.reshape(row_count, head_count, head_size)
    key_rows = lin_key.reshape(row_count, head_count, head_size)
    value_rows = lin_value.reshape(row_count, head_count, head_size)
    order = jnp.arange(row_count, dtype=jnp.int32)
    lower_mask = order[:, None] >= order[None, :]
    cum_decay = jnp.dot(
        log_decay, lower_mask.T.astype(jnp.float32), precision=lax.Precision.HIGHEST
    )
    same_doc = lower_mask & (doc_ids[:, None] == doc_ids[None, :])
    log_gap = jnp.minimum(cum_decay[:, :, None] - cum_decay[:, None, :], 0.0)
    decay_matrix = jnp.where(same_doc[None], jnp.exp(log_gap), 0.0)
    scores = jnp.einsum("thd,shd->hts", queries, key_rows, preferred_element_type=jnp.float32)
    weights = (scores * decay_matrix).astype(jnp.bfloat16)
    local_term = jnp.einsum("hts,shd->thd", weights, value_rows, preferred_element_type=jnp.float32)
    last_cum = cum_decay[:, -1]
    tail_weight = (
        jnp.exp(last_cum[:, None] - cum_decay)
        * (doc_ids == doc_ids[-1]).astype(jnp.float32)[None, :]
    )
    scaled_keys = key_rows.astype(jnp.float32) * tail_weight.T[:, :, None]
    block_state = jnp.einsum(
        "shd,she->hde", scaled_keys, value_rows.astype(jnp.float32), precision=lax.Precision.HIGHEST
    )
    carry_factor = jnp.exp(last_cum) * (doc_ids[-1] == prev_doc).astype(jnp.float32)
    identity = (jnp.ones_like(carry_factor), jnp.zeros_like(block_state))
    _, incoming = entering((carry_factor, block_state), "ctx", chain_combine, identity)
    continues = (doc_ids == prev_doc).astype(jnp.float32)
    entry_weight = jnp.exp(cum_decay).T * continues[:, None]
    carried_term = (
        jnp.einsum(
            "thd,hde->the", queries.astype(jnp.float32), incoming, precision=lax.Precision.HIGHEST
        )
        * entry_weight[:, :, None]
    )
    attention = (local_term + carried_term).reshape(row_count, features)
    square_sums = jnp.sum(attention * attention, axis=1)
    total_squares = lax.psum(square_sums, "tp")
    mean_square = total_squares / (HEADS * HEAD_DIM)
    gated = jax.nn.sigmoid(out_gate.astype(jnp.float32))
    return (
        attention * lax.rsqrt(mean_square + norm_epsilon)[:, None] * norm_gain[None, :] * gated
    ).astype(jnp.bfloat16)


def project_values(lin_out, value_proj):
    row_count = lin_out.shape[0]
    group_count = value_proj.shape[0]
    grouped = lin_out.reshape(row_count, group_count, -1)
    projected = jnp.einsum("tgf,gfe->tge", grouped, value_proj, preferred_element_type=jnp.float32)
    return projected.astype(jnp.bfloat16).reshape(row_count, group_count * value_proj.shape[2])


def softmax_section(soft_query, soft_key, values, doc_lengths, active):
    row_count, features = soft_query.shape
    group_count = soft_key.shape[1] // HEAD_DIM
    per_group = features // (group_count * HEAD_DIM)
    query_grid = soft_query.reshape(row_count, group_count, per_group, HEAD_DIM)
    first_pos = lax.axis_index("ctx") * row_count
    token_positions = first_pos + jnp.arange(row_count, dtype=jnp.int32)
    query_docs = doc_numbers(doc_lengths, token_positions)
    scale = 1.0 / math.sqrt(HEAD_DIM)
    initial = (
        jnp.full((group_count, per_group, row_count), -1e30, jnp.float32),
        jnp.zeros((group_count, per_group, row_count), jnp.float32),
        jnp.zeros((group_count, per_group, row_count, HEAD_DIM), jnp.float32),
    )
    key_rows = lax.all_gather(soft_key, "ctx", axis=0, tiled=True)
    value_rows = lax.all_gather(values, "ctx", axis=0, tiled=True)
    count = key_rows.shape[0]
    block = math.gcd(count, 1024)
    block_count = count // block
    key_blocks = key_rows.reshape(block_count, block, group_count, HEAD_DIM)
    value_blocks = value_rows.reshape(block_count, block, group_count, HEAD_DIM)
    offsets = block * jnp.arange(block_count, dtype=jnp.int32)

    def one_block(state_now, inputs):
        key_block, value_block, offset = inputs
        key_pos = offset + jnp.arange(block, dtype=jnp.int32)
        key_docs = doc_numbers(doc_lengths, key_pos)
        allowed = (key_pos[None, :] <= token_positions[:, None]) & (
            key_docs[None, :] == query_docs[:, None]
        )

        def update(state_in):
            running, total, accum = state_in
            scores = (
                jnp.einsum(
                    "tgcd,sgd->gcts", query_grid, key_block, preferred_element_type=jnp.float32
                )
                * scale
            )
            masked = jnp.where(allowed, scores, -1e30)
            new_top = jnp.maximum(running, jnp.max(masked, axis=-1))
            factor = jnp.exp(running - new_top)
            probs = jnp.where(allowed, jnp.exp(scores - new_top[..., None]), 0.0)
            total = total * factor + jnp.sum(probs, axis=-1)
            accum = accum * factor[..., None] + jnp.einsum(
                "gcts,sgd->gctd",
                probs.astype(jnp.bfloat16),
                value_block,
                preferred_element_type=jnp.float32,
            )
            return (new_top, total, accum)

        def keep_state(state_in):
            return state_in

        result = lax.cond(active, update, keep_state, state_now)
        return (result, None)

    final_state, _ = lax.scan(one_block, initial, (key_blocks, value_blocks, offsets))
    _, total, accum = final_state
    result = accum / jnp.maximum(total, 1.0)[..., None]
    return result.transpose(2, 0, 1, 3).reshape(row_count, features).astype(jnp.bfloat16)


def local(
    lin_query,
    lin_key,
    lin_value,
    log_decay,
    out_gate,
    norm_gain,
    value_proj,
    soft_query,
    soft_key,
    doc_lengths,
):
    segment = lax.axis_index("pipe")
    active = segment == 1
    phase_query = jnp.where(active, jnp.zeros_like(lin_query), lin_query)
    lin_out = lightning_section(
        phase_query, lin_key, lin_value, log_decay, out_gate, norm_gain, doc_lengths
    )
    arrived = shifted(lin_out, "pipe", 1)
    soft_values = project_values(arrived, value_proj)
    soft_out = softmax_section(soft_query, soft_key, soft_values, doc_lengths, active)
    return jnp.where(segment == 0, lin_out, soft_out)[None]


def solution(mesh):
    return jax.shard_map(
        local,
        mesh=mesh,
        in_specs=(
            P("ctx", "tp"),
            P("ctx", "tp"),
            P("ctx", "tp"),
            P("tp", "ctx"),
            P("ctx", "tp"),
            P("tp"),
            P("tp", None, None),
            P("ctx", "tp"),
            P("ctx", "tp"),
            P(),
        ),
        out_specs=P("pipe", "ctx", "tp"),
        check_vma=False,
    )
```

profile of v0, /device:TPU:230, one launch (start us, length us, event | category | flops | bytes accessed | tf_op | source)
XLA Modules:
  0.0 871.7 jit_solution(12368734724042462260)
XLA Ops:
  12.0 4.2 fusion.27
  18.5 190.1 %all-reduce = f32[1024]{0:T(1024)S(1)} all-reduce(f32[1024]{0:T(1024)S(1)} %dynamic-update-slice), channel_id=2, replica_groups=mesh['pipe'=2,'ctx'=64,'tp'=2] {'ctx'}, use_global_device_ids=true, to_apply=%add | all-reduce | flops 1024 | bytes 8192
  210.9 330.9 %all-gather.10.cloned.1.call-done = f32[1024,128,128]{2,1,0:T(8,128)} async-done(((f32[16,128,128]{2,1,0:T(8,128)}), f32[1024,128,128]{2,1,0:T(8,128)}) %all-gather.10.cloned.1.call-update) | async-done | bytes 67108880 | tf_op jit(solution)/shard_map/all_gather | solution.py:17
  541.9 90.2 %while.29 = (s32[]{:T(128)}, f32[16,128,128]{2,1,0:T(8,128)S(1)}, s32[]{:T(128)}, f32[64,16]{1,0:T(8,128)S(1)}, f32[64,16,128,128]{3,2,1,0:T(8,128)}, /*index=5*/s32[]{:T(128)}, s32[]{:T(128)}, s32[]{:T(128)}) while((s32[]{:T(128)}, f32[16,128,128]{2,1,0:T(8,128)S(1)}, s32[]{:T(128)}, f32[64,16]{1,0:T(8,128)S(1)}, ...), condition=%wide.region_4.5_spmd, body=%wide.region_3.4_spmd.sunk | while | flops 524293 | bytes 3146047 | solution.py:25
  639.9 15.8 %collective-permute-done = bf16[144,2048]{1,0:T(8,128)(2,1)S(1)} collective-permute-done((bf16[144,2048]{1,0:T(8,128)(2,1)S(1)}, bf16[144,2048]{1,0:T(8,128)(2,1)S(1)}, u32[]{:S(2)}, u32[]{:S(2)}) %collective-permute-start) | collective-permute-done | bytes 589856 | tf_op jit(solution)/shard_map/ppermute | solution.py:31
  658.3 7.7 reshape.161
  665.9 5.4 copy.49
  671.4 78.6 %all-gather.8.cloned.1.call-done = bf16[9216,256]{1,0:T(8,128)(2,1)} async-done(((bf16[144,256]{1,0:T(8,128)(2,1)}), bf16[9216,256]{1,0:T(8,128)(2,1)}) %all-gather.8.cloned.1.call-update) | async-done | bytes 4718608 | tf_op jit(solution)/shard_map/all_gather | solution.py:119
  750.0 7.7 reshape.165
  757.7 5.5 copy.51
  763.3 100.3 %while.30 = (s32[]{:T(128)}, f32[2,8,144]{2,1,0:T(8,128)S(1)}, f32[2,8,144]{2,1,0:T(8,128)S(1)}, f32[2,8,144,128]{3,2,1,0:T(8,128)S(1)}, pred[]{:T(512)}, /*inde...) while((s32[]{:T(128)}, f32[2,8,144]{2,1,0:T(8,128)S(1)}, ...), condition=%wide.region_14.15_spmd.clone, body=%wide.region_8.14_spmd.clone.sunk | while | flops 1234974336 | bytes 33149084 | solution.py:162
  764.7 9.8 %conditional.3 = ((f32[2,8,144]{2,1,0:T(8,128)S(1)}, f32[2,8,144]{2,1,0:T(8,128)S(1)}, f32[2,8,144,128]{3,2,1,0:T(8,128)S(1)})) conditional(s32[]{:T(128)} %convert_element_type.123, (f32[2,8,144]{2,1,0:T(8,128)S(1)}, f32[2,8,144]{2,1,0:T(8,128)S(1)}, f32[2,8,144,128]{3,2,1,0:T(8,128)S(1)}) %tuple.70, (s32[]{:T(128)}, s32[1,1024]{1,0:T(1,128)S(1)}, ...), branch_computations={%region_9.9_spmd, %region_10.13_spmd} | conditional | flops 1234956928 | bytes 33103148 | solution.py:159
  771.0 3.4 fusion.10
  775.8 9.8 %conditional.3 = ((f32[2,8,144]{2,1,0:T(8,128)S(1)}, f32[2,8,144]{2,1,0:T(8,128)S(1)}, f32[2,8,144,128]{3,2,1,0:T(8,128)S(1)})) conditional(s32[]{:T(128)} %convert_element_type.123, (f32[2,8,144]{2,1,0:T(8,128)S(1)}, f32[2,8,144]{2,1,0:T(8,128)S(1)}, f32[2,8,144,128]{3,2,1,0:T(8,128)S(1)}) %tuple.70, (s32[]{:T(128)}, s32[1,1024]{1,0:T(1,128)S(1)}, ...), branch_computations={%region_9.9_spmd, %region_10.13_spmd} | conditional | flops 1234956928 | bytes 33103148 | solution.py:159
  782.2 3.4 fusion.10
  787.0 9.8 %conditional.3 = ((f32[2,8,144]{2,1,0:T(8,128)S(1)}, f32[2,8,144]{2,1,0:T(8,128)S(1)}, f32[2,8,144,128]{3,2,1,0:T(8,128)S(1)})) conditional(s32[]{:T(128)} %convert_element_type.123, (f32[2,8,144]{2,1,0:T(8,128)S(1)}, f32[2,8,144]{2,1,0:T(8,128)S(1)}, f32[2,8,144,128]{3,2,1,0:T(8,128)S(1)}) %tuple.70, (s32[]{:T(128)}, s32[1,1024]{1,0:T(1,128)S(1)}, ...), branch_computations={%region_9.9_spmd, %region_10.13_spmd} | conditional | flops 1234956928 | bytes 33103148 | solution.py:159
  798.1 9.8 %conditional.3 = ((f32[2,8,144]{2,1,0:T(8,128)S(1)}, f32[2,8,144]{2,1,0:T(8,128)S(1)}, f32[2,8,144,128]{3,2,1,0:T(8,128)S(1)})) conditional(s32[]{:T(128)} %convert_element_type.123, (f32[2,8,144]{2,1,0:T(8,128)S(1)}, f32[2,8,144]{2,1,0:T(8,128)S(1)}, f32[2,8,144,128]{3,2,1,0:T(8,128)S(1)}) %tuple.70, (s32[]{:T(128)}, s32[1,1024]{1,0:T(1,128)S(1)}, ...), branch_computations={%region_9.9_spmd, %region_10.13_spmd} | conditional | flops 1234956928 | bytes 33103148 | solution.py:159
  804.5 3.4 fusion.10
  809.3 9.8 %conditional.3 = ((f32[2,8,144]{2,1,0:T(8,128)S(1)}, f32[2,8,144]{2,1,0:T(8,128)S(1)}, f32[2,8,144,128]{3,2,1,0:T(8,128)S(1)})) conditional(s32[]{:T(128)} %convert_element_type.123, (f32[2,8,144]{2,1,0:T(8,128)S(1)}, f32[2,8,144]{2,1,0:T(8,128)S(1)}, f32[2,8,144,128]{3,2,1,0:T(8,128)S(1)}) %tuple.70, (s32[]{:T(128)}, s32[1,1024]{1,0:T(1,128)S(1)}, ...), branch_computations={%region_9.9_spmd, %region_10.13_spmd} | conditional | flops 1234956928 | bytes 33103148 | solution.py:159
  820.4 9.8 %conditional.3 = ((f32[2,8,144]{2,1,0:T(8,128)S(1)}, f32[2,8,144]{2,1,0:T(8,128)S(1)}, f32[2,8,144,128]{3,2,1,0:T(8,128)S(1)})) conditional(s32[]{:T(128)} %convert_element_type.123, (f32[2,8,144]{2,1,0:T(8,128)S(1)}, f32[2,8,144]{2,1,0:T(8,128)S(1)}, f32[2,8,144,128]{3,2,1,0:T(8,128)S(1)}) %tuple.70, (s32[]{:T(128)}, s32[1,1024]{1,0:T(1,128)S(1)}, ...), branch_computations={%region_9.9_spmd, %region_10.13_spmd} | conditional | flops 1234956928 | bytes 33103148 | solution.py:159
  831.6 9.8 %conditional.3 = ((f32[2,8,144]{2,1,0:T(8,128)S(1)}, f32[2,8,144]{2,1,0:T(8,128)S(1)}, f32[2,8,144,128]{3,2,1,0:T(8,128)S(1)})) conditional(s32[]{:T(128)} %convert_element_type.123, (f32[2,8,144]{2,1,0:T(8,128)S(1)}, f32[2,8,144]{2,1,0:T(8,128)S(1)}, f32[2,8,144,128]{3,2,1,0:T(8,128)S(1)}) %tuple.70, (s32[]{:T(128)}, s32[1,1024]{1,0:T(1,128)S(1)}, ...), branch_computations={%region_9.9_spmd, %region_10.13_spmd} | conditional | flops 1234956928 | bytes 33103148 | solution.py:159
  837.9 3.4 fusion.10
  842.7 9.8 %conditional.3 = ((f32[2,8,144]{2,1,0:T(8,128)S(1)}, f32[2,8,144]{2,1,0:T(8,128)S(1)}, f32[2,8,144,128]{3,2,1,0:T(8,128)S(1)})) conditional(s32[]{:T(128)} %convert_element_type.123, (f32[2,8,144]{2,1,0:T(8,128)S(1)}, f32[2,8,144]{2,1,0:T(8,128)S(1)}, f32[2,8,144,128]{3,2,1,0:T(8,128)S(1)}) %tuple.70, (s32[]{:T(128)}, s32[1,1024]{1,0:T(1,128)S(1)}, ...), branch_computations={%region_9.9_spmd, %region_10.13_spmd} | conditional | flops 1234956928 | bytes 33103148 | solution.py:159
  853.9 9.8 %conditional.3 = ((f32[2,8,144]{2,1,0:T(8,128)S(1)}, f32[2,8,144]{2,1,0:T(8,128)S(1)}, f32[2,8,144,128]{3,2,1,0:T(8,128)S(1)})) conditional(s32[]{:T(128)} %convert_element_type.123, (f32[2,8,144]{2,1,0:T(8,128)S(1)}, f32[2,8,144]{2,1,0:T(8,128)S(1)}, f32[2,8,144,128]{3,2,1,0:T(8,128)S(1)}) %tuple.70, (s32[]{:T(128)}, s32[1,1024]{1,0:T(1,128)S(1)}, ...), branch_computations={%region_9.9_spmd, %region_10.13_spmd} | conditional | flops 1234956928 | bytes 33103148 | solution.py:159
  (306 shorter events, 193.5 us)
Async XLA Ops:
  6.5 5.4 copy-start
  6.5 10.5 %copy-start.6 = (u32[256]{0:T(256)S(1)}, u32[256]{0:T(256)}, u32[]{:S(2)}) copy-start(u32[256]{0:T(256)} %constant.110) | copy-start | bytes 3076
  6.5 202.2 %copy-start.3 = (bf16[144,2048]{1,0:T(8,128)(2,1)S(1)}, bf16[144,2048]{1,0:T(8,128)(2,1)}, u32[]{:S(2)}) copy-start(bf16[144,2048]{1,0:T(8,128)(2,1)} %param.17) | copy-start | bytes 1769476
  6.5 202.2 %copy-start.1 = (bf16[144,2048]{1,0:T(8,128)(2,1)S(1)}, bf16[144,2048]{1,0:T(8,128)(2,1)}, u32[]{:S(2)}) copy-start(bf16[144,2048]{1,0:T(8,128)(2,1)} %param.16) | copy-start | bytes 1769476
  6.5 535.3 %all-gather.10.cloned.1.call-start = ((), (), s32[]{:S(2)}) async-start(), calls=%async_computation.2 | async-start | bytes 68157440 | tf_op jit(solution)/shard_map/all_gather | solution.py:17
  16.2 642.1 %all-gather.6.cloned.1.call-start = ((), (), s32[]{:S(2)}) async-start(), calls=%async_computation | async-start | bytes 4792320 | tf_op jit(solution)/shard_map/all_gather | solution.py:118
  17.0 733.1 %all-gather.8.cloned.1.call-start = ((), (), s32[]{:S(2)}) async-start(), calls=%async_computation.1 | async-start | bytes 4792320 | tf_op jit(solution)/shard_map/all_gather | solution.py:119
  632.1 4.9 copy-start.4
  634.4 23.4 %copy-start.2 = (bf16[144,2048]{1,0:T(8,128)(2,1)S(1)}, bf16[144,2048]{1,0:T(8,128)(2,1)}, u32[]{:S(2)}) copy-start(bf16[144,2048]{1,0:T(8,128)(2,1)} %param.23) | copy-start | bytes 1769476
  638.4 19.6 %copy-start.5 = (s32[8]{0:T(128)S(1)}, s32[8]{0:T(128)}, u32[]{:S(2)}) copy-start(s32[8]{0:T(128)} %param.25) | copy-start | bytes 100
  638.4 17.3 %collective-permute-start = (bf16[144,2048]{1,0:T(8,128)(2,1)S(1)}, bf16[144,2048]{1,0:T(8,128)(2,1)S(1)}, u32[]{:S(2)}, u32[]{:S(2)}) collective-permute-start(bf16[144,2048]{1,0:T(8,128)(2,1)S(1)} %fusion.26), channel_id=1, source_target_pairs={{0,128},{1,129},{2,130},{3,131},{4,132},{5,133},{6,134},{7,135},{8... | collective-permute-start | bytes 1769480 | tf_op jit(solution)/shard_map/ppermute | solution.py:31
Sparse Core Ops, SparseCore 0:
  16.3 525.4 all-gather.9
  545.0 87.9 all-gather.5
  657.9 92.0 all-gather.7
where the time goes:
time: 879 us; the launch traced here: 872 us
  waiting for transfers between devices  426 us (48%)
  blocking collectives  193 us (22%)
  other arithmetic  130 us (15%)
  matrix products  66.8 us (8%)
  local copies, waits for them, and re-layouts  35.5 us (4%)
  between operations  15.3 us (2%)
    all_gather x1, waiting for transfers between devices, entering(): gathered = jax.tree.map(lambda a: lax.all_gather(a, axis), part)  331 us
    unnamed x1, blocking collectives  190 us
    add x60, other arithmetic, chain_combine(): later[0][:, None, None] * earlier[1] + later[1]  87.2 us
    all_gather x1, waiting for transfers between devices, softmax_section(): value_rows = lax.all_gather(values, 'ctx', axis=0, tiled=True)  78.6 us
    dot_general x9, matrix products, update(): jnp.einsum('gcts,sgd->gctd', probs.astype(jnp.bfloat16), value_block, pre...  30.6 us
    dot_general x9, matrix products, update(): jnp.einsum('tgcd,sgd->gcts', query_grid, key_block, preferred_element_typ...  25.4 us
    reduce_sum x9, other arithmetic, update(): total = total * factor + jnp.sum(probs, axis=-1)  23.5 us
  transfers between devices with their start and end apart: 4, of which 3 were waited for; matrix products, arithmetic and copies ran while one was open for 13% of the time, Pallas kernels for 0%

commit v1 on v0

v1 whole, which is shorter than its diff:
```python
import math

import jax
import jax.numpy as jnp
from jax import lax
from jax.experimental import pallas as pl
from jax.experimental.pallas import tpu as pltpu
from jax.sharding import PartitionSpec as P

MESH = pl.DeviceIdType.MESH
ALL_HEADS = 32
DIM = 128
ROWS = 144
HEADS = 8
WIDTH = HEADS * DIM
DOCS = 8
EPSILON = 1e-06
F32 = jnp.float32
BF16 = jnp.bfloat16


def place():
    ctx = lax.axis_index("ctx")
    return (
        lax.axis_index("pipe"),
        lax.div(ctx, 16),
        lax.rem(lax.div(ctx, 4), 4),
        lax.rem(ctx, 4),
        lax.axis_index("tp"),
    )


def doc_starts(docs, positions):
    end = jnp.int32(0)
    start = jnp.zeros_like(positions)
    for i in range(DOCS):
        end = end + docs[i]
        start = jnp.where(end <= positions, end, start)
    return start


def halves(x):
    high = x.astype(BF16)
    return high, (x - high.astype(F32)).astype(BF16)


def thirds(x):
    high = x.astype(BF16)
    rest = x - high.astype(F32)
    mid = rest.astype(BF16)
    return high, mid, (rest - mid.astype(F32)).astype(BF16)


def matmul(a, b, ca, cb):
    return lax.dot_general(a, b, (((ca,), (cb,)), ((), ())), preferred_element_type=F32)


def section_kernel(
    lq, lk, lv, ld, og, gain, vp, sk, docs,
    lin_out, kall, vall,
    qb, kb, vb, ldb, ogb, gb, vpb,
    bst, ybuf, ypre, yfac, tsend, xbuf, xpre, xfac, zsend, zbuf, xsend, xin, ysend, yin,
    loc, sqb,
    load_sem, ksend, krecv, vsend, vrecv, ssend, srecv, qsend, qrecv,
):
    p, z, x, y, t = place()
    ctx = z * 16 + x * 4 + y
    first = ctx * ROWS

    columns = pl.ds(pl.multiple_of(p * WIDTH, WIDTH), WIDTH)
    loads = [
        pltpu.make_async_copy(src, dst, load_sem.at[i])
        for i, (src, dst) in enumerate((
            (sk.at[:, pl.ds(pl.multiple_of(p * DIM, DIM), DIM)], kall.at[z, x, y]),
            (ld.at[pl.ds(pl.multiple_of(p * HEADS, HEADS), HEADS)], ldb),
            (lk.at[:, columns], kb),
            (lv.at[:, columns], vb),
            (lq.at[:, columns], qb),
            (og.at[:, columns], ogb),
            (gain.at[:, columns], gb),
            (vp.at[p], vpb),
        ))
    ]
    for load in loads:
        load.start()

    def y_peer(d):
        return (p, z * 16 + x * 4 + lax.rem(y + d, 4), t)

    def x_peer(d):
        return (p, z * 16 + lax.rem(x + d, 4) * 4 + y, t)

    def z_peer(d):
        return (p, lax.rem(z + d, 4) * 16 + x * 4 + y, t)

    quad = [(1 - p, ctx, t), (p, ctx, 1 - t), (1 - p, ctx, 1 - t)]

    barrier = pltpu.get_barrier_semaphore()
    for d in (1, 2, 3):
        for peer in (y_peer(d), x_peer(d), z_peer(d), quad[d - 1]):
            pl.semaphore_signal(barrier, inc=1, device_id=peer, device_id_type=MESH)
    pl.semaphore_wait(barrier, 12)

    def remote(src, dst, send, recv, i, peer):
        return pltpu.make_async_remote_copy(
            src_ref=src, dst_ref=dst, send_sem=send.at[i], recv_sem=recv.at[i],
            device_id=peer, device_id_type=MESH,
        )

    started = []

    def start(copies):
        for copy in copies:
            copy.start()
        started.extend(copies)
        return copies

    def arrived(copies):
        for copy in copies:
            copy.wait_recv()

    def gather_z(buf, send, recv):
        mine = buf.at[z, x, y]
        return start([remote(mine, mine, send, recv, d - 1, z_peer(d)) for d in (1, 2, 3)])

    def gather_x(buf, send, recv):
        mine = buf.at[:, x, y]
        return start([remote(mine, mine, send, recv, d + 2, x_peer(d)) for d in (1, 2, 3)])

    def gather_y(buf, send, recv):
        mine = buf.at[:, :, y]
        return start([remote(mine, mine, send, recv, d + 5, y_peer(d)) for d in (1, 2, 3)])

    loads[0].wait()
    phase_k = gather_z(kall, ksend, krecv)

    row = lax.broadcasted_iota(jnp.int32, (ROWS, ROWS), 0)
    col = lax.broadcasted_iota(jnp.int32, (ROWS, ROWS), 1)
    begin = doc_starts(docs, first + lax.broadcasted_iota(jnp.int32, (ROWS, 1), 0)) - first
    last_begin = doc_starts(docs, jnp.full((1, 1), first + ROWS - 1, jnp.int32)) - first
    lower = (row >= col).astype(F32).astype(BF16)
    same_doc = (row >= col) & (col >= begin)
    continues = (begin < 0).astype(F32)
    last_continues = (last_begin < 0).astype(F32)
    in_last = (lax.broadcasted_iota(jnp.int32, (ROWS, 1), 0) >= last_begin).astype(F32)

    loads[1].wait()
    pieces = thirds(ldb[...])
    cum_row = sum(matmul(a, lower, 1, 1) for a in pieces)
    cum_col = sum(matmul(lower, a, 1, 1) for a in pieces)

    loads[2].wait()
    loads[3].wait()
    for h in range(HEADS):
        cols = slice(h * DIM, (h + 1) * DIM)
        last = cum_row[h : h + 1, ROWS - 1 : ROWS]
        tail = jnp.exp(last - cum_col[:, h : h + 1]) * in_last
        parts = halves(vb[:, cols].astype(F32) * tail)
        state = matmul(kb[:, cols], jnp.concatenate(parts, axis=1), 0, 0)
        bst[h, 0:DIM, :] = state[:, :DIM] + state[:, DIM:]
        bst[h, DIM : DIM + 8, :] = jnp.broadcast_to(jnp.exp(last) * last_continues, (8, DIM))

    phase = start([
        remote(bst.at[pl.ds(2 * lax.rem(y + d, 4), 2)], ybuf.at[y], ssend, srecv, d - 1, y_peer(d))
        for d in (1, 2, 3)
    ])
    ybuf[y] = bst[pl.ds(2 * y, 2)]

    arrived(phase_k)
    phase_k = gather_x(kall, ksend, krecv)

    loads[4].wait()
    for h in range(HEADS):
        cols = slice(h * DIM, (h + 1) * DIM)
        scores = matmul(qb[:, cols], kb[:, cols], 1, 1)
        gap = jnp.minimum(cum_col[:, h : h + 1] - cum_row[h : h + 1, :], 0.0)
        weights = (scores * jnp.where(same_doc, jnp.exp(gap), 0.0)).astype(BF16)
        loc[:, cols] = matmul(weights, vb[:, cols], 1, 0)

    arrived(phase)
    for i in range(2):
        prefix = jnp.zeros((DIM, DIM), F32)
        factor = jnp.ones((8, DIM), F32)
        for k in range(4):
            ypre[k, i] = prefix
            yfac[k, i] = factor
            f = ybuf[k, i, DIM : DIM + 8, :]
            prefix = prefix * f[0:1] + ybuf[k, i, 0:DIM, :]
            factor = factor * f
        tsend[2 * i, 0:64] = prefix[0:64]
        tsend[2 * i + 1, 0:64] = prefix[64:128]
        tsend[2 * i, 64:72] = factor
        tsend[2 * i + 1, 64:72] = factor

    phase = start([
        remote(tsend.at[lax.rem(x + d, 4)], xbuf.at[x], ssend, srecv, d + 2, x_peer(d))
        for d in (1, 2, 3)
    ])
    xbuf[x] = tsend[x]
    arrived(phase)
    prefix = jnp.zeros((64, DIM), F32)
    factor = jnp.ones((8, DIM), F32)
    for k in range(4):
        xpre[k] = prefix
        xfac[k] = factor
        f = xbuf[k, 64:72, :]
        prefix = prefix * f[0:1] + xbuf[k, 0:64, :]
        factor = factor * f
    zsend[0:64] = prefix
    zsend[64:72] = factor

    phase = start([
        remote(zsend, zbuf.at[z], ssend, srecv, d + 5, z_peer(d)) for d in (1, 2, 3)
    ])
    zbuf[z] = zsend[...]
    arrived(phase_k)
    phase_k = gather_y(kall, ksend, krecv)
    arrived(phase)
    state = jnp.zeros((64, DIM), F32)
    for k in range(3):
        state = jnp.where(k < z, state * zbuf[k, 64:65, :] + zbuf[k, 0:64, :], state)
    for k in range(4):
        xsend[k] = state * xfac[k, 0:1] + xpre[k]

    phase = start([
        remote(xsend.at[lax.rem(x + d, 4)], xin.at[x], ssend, srecv, d + 8, x_peer(d))
        for d in (1, 2, 3)
    ])
    xin[x] = xsend[x]
    arrived(phase)
    for i in range(2):
        for half in range(2):
            state = xin[2 * i + half]
            span = slice(half * 64, half * 64 + 64)
            for k in range(4):
                ysend[k, i, span] = state * yfac[k, i, 0:1] + ypre[k, i, span]

    phase = start([
        remote(ysend.at[lax.rem(y + d, 4)], yin.at[y], ssend, srecv, d + 11, y_peer(d))
        for d in (1, 2, 3)
    ])
    yin[y] = ysend[y]
    arrived(phase)

    squares = jnp.zeros((ROWS, DIM), F32)
    for h in range(HEADS):
        cols = slice(h * DIM, (h + 1) * DIM)
        parts = halves(yin[h // 2, h % 2])
        carried = matmul(qb[:, cols], jnp.concatenate(parts, axis=1), 1, 0)
        weight = jnp.exp(cum_col[:, h : h + 1]) * continues
        attention = loc[:, cols] + weight * (carried[:, :DIM] + carried[:, DIM:])
        loc[:, cols] = attention
        squares = squares + attention * attention

    eye = row == col
    total = jnp.sum(squares, axis=1, keepdims=True)
    sqb[0] = jnp.broadcast_to(jnp.sum(jnp.where(eye, total, 0.0), axis=0, keepdims=True), (8, ROWS))
    phase = start([
        remote(sqb.at[0], sqb.at[i + 1], qsend, qrecv, i, quad[i]) for i in range(3)
    ])
    for load in loads[5:]:
        load.wait()
    arrived(phase)
    total = sqb[0, 0:1] + sqb[1, 0:1] + (sqb[2, 0:1] + sqb[3, 0:1])
    total = jnp.sum(jnp.where(eye, total, 0.0), axis=1, keepdims=True)
    scale = lax.rsqrt(total / (ALL_HEADS * DIM) + EPSILON)
    for h in range(HEADS):
        cols = slice(h * DIM, (h + 1) * DIM)
        gate = jax.nn.sigmoid(ogb[:, cols].astype(F32))
        lin_out[:, cols] = (loc[:, cols] * scale * gb[:, cols] * gate).astype(BF16)
    vall[z, x, y] = matmul(lin_out[...], vpb[...], 1, 0).astype(BF16)

    phase_v = gather_z(vall, vsend, vrecv)
    arrived(phase_k)
    arrived(phase_v)
    phase_v = gather_x(vall, vsend, vrecv)
    arrived(phase_v)
    phase_v = gather_y(vall, vsend, vrecv)
    arrived(phase_v)
    for copy in started:
        copy.wait_send()


def section(lq, lk, lv, ld, og, gain, vp, sk, docs):
    anywhere = pl.BlockSpec(memory_space=pl.ANY)
    vmem = pl.BlockSpec(memory_space=pltpu.VMEM)
    gathered = jax.ShapeDtypeStruct((4, 4, 4, ROWS, DIM), BF16)
    dma = pltpu.SemaphoreType.DMA
    return pl.pallas_call(
        section_kernel,
        out_shape=(jax.ShapeDtypeStruct((ROWS, WIDTH), BF16), gathered, gathered),
        in_specs=[anywhere] * 8 + [pl.BlockSpec(memory_space=pltpu.SMEM)],
        out_specs=(vmem, vmem, vmem),
        scratch_shapes=[
            pltpu.VMEM((ROWS, WIDTH), BF16),
            pltpu.VMEM((ROWS, WIDTH), BF16),
            pltpu.VMEM((ROWS, WIDTH), BF16),
            pltpu.VMEM((HEADS, ROWS), F32),
            pltpu.VMEM((ROWS, WIDTH), BF16),
            pltpu.VMEM((1, WIDTH), F32),
            pltpu.VMEM((WIDTH, DIM), BF16),
            pltpu.VMEM((HEADS, DIM + 8, DIM), F32),
            pltpu.VMEM((4, 2, DIM + 8, DIM), F32),
            pltpu.VMEM((4, 2, DIM, DIM), F32),
            pltpu.VMEM((4, 2, 8, DIM), F32),
            pltpu.VMEM((4, 72, DIM), F32),
            pltpu.VMEM((4, 72, DIM), F32),
            pltpu.VMEM((4, 64, DIM), F32),
            pltpu.VMEM((4, 8, DIM), F32),
            pltpu.VMEM((72, DIM), F32),
            pltpu.VMEM((4, 72, DIM), F32),
            pltpu.VMEM((4, 64, DIM), F32),
            pltpu.VMEM((4, 64, DIM), F32),
            pltpu.VMEM((4, 2, DIM, DIM), F32),
            pltpu.VMEM((4, 2, DIM, DIM), F32),
            pltpu.VMEM((ROWS, WIDTH), F32),
            pltpu.VMEM((4, 8, ROWS), F32),
            dma((8,)), dma((9,)), dma((9,)), dma((9,)), dma((9,)), dma((15,)), dma((15,)), dma((3,)), dma((3,)),
        ],
        compiler_params=pltpu.CompilerParams(
            collective_id=0, has_side_effects=True, vmem_limit_bytes=40 << 20
        ),
        name="section",
    )(lq, lk, lv, ld, og, gain, vp, sk, docs)


CHUNK = 256
BAND = 2
SLOPE = math.log2(math.e) / math.sqrt(DIM)


def softmax_kernel(sq, keys, values, docs, out, queries, top, total, accum, load_sem):
    p = lax.axis_index("pipe")
    first = lax.axis_index("ctx") * ROWS
    loads = [
        pltpu.make_async_copy(
            sq.at[:, pl.ds(pl.multiple_of(p * WIDTH + h * DIM, DIM), DIM)],
            queries.at[h // BAND, pl.ds((h % BAND) * ROWS, ROWS)],
            load_sem.at[h],
        )
        for h in range(HEADS)
    ]
    for load in loads:
        load.start()
    start = jnp.int32(0)
    latest = jnp.int32(0)
    end = jnp.int32(0)
    for i in range(DOCS):
        end = end + docs[i]
        start = jnp.where(end <= first, end, start)
        latest = jnp.where(end <= first + ROWS - 1, end, latest)
    begin_chunk = lax.div(start, CHUNK)
    end_chunk = lax.div(first + ROWS - 1, CHUNK) + 1
    full_from = jnp.minimum(lax.div(latest + CHUNK - 1, CHUNK), end_chunk)
    full_to = jnp.maximum(lax.div(first + 1, CHUNK), full_from)
    row = lax.rem(lax.broadcasted_iota(jnp.int32, (BAND * ROWS, 1), 0), ROWS) + first
    begin = doc_starts(docs, row)
    for load in loads:
        load.wait()
    top[...] = jnp.full_like(top, -1e30)
    total[...] = jnp.zeros_like(total)
    accum[...] = jnp.zeros_like(accum)

    def score(band, chunk, masked):
        at = pl.multiple_of(chunk * CHUNK, CHUNK)
        scores = matmul(queries[band], keys[pl.ds(at, CHUNK)], 1, 1)
        if masked:
            position = at + lax.broadcasted_iota(jnp.int32, (1, CHUNK), 1)
            scores = jnp.where((position <= row) & (position >= begin), scores, -1e30)
        return scores

    def fold(s, op):
        parts = [s[:, i : i + DIM] for i in range(0, CHUNK, DIM)]
        while len(parts) > 1:
            parts = [op(a, b) for a, b in zip(parts[::2], parts[1::2])]
        return parts[0]

    def find(chunk, masked):
        for band in range(HEADS // BAND):
            top[band] = jnp.maximum(top[band], fold(score(band, chunk, masked), jnp.maximum))

    def add(chunk, masked):
        at = pl.multiple_of(chunk * CHUNK, CHUNK)
        for band in range(HEADS // BAND):
            scores = score(band, chunk, masked)
            probs = jnp.exp2((scores - top[band][:, 0:1]) * SLOPE)
            total[band] += fold(probs, jnp.add)
            accum[band] += matmul(probs.astype(BF16), values[pl.ds(at, CHUNK)], 1, 0)

    def over(step):
        for low, high, masked in (
            (begin_chunk, full_from, True),
            (full_from, full_to, False),
            (full_to, end_chunk, True),
        ):
            @pl.loop(jnp.int32(low), jnp.int32(high))
            def _(chunk):
                step(chunk, masked)

    over(find)
    for band in range(HEADS // BAND):
        top[band] = jnp.broadcast_to(
            jnp.max(top[band], axis=1, keepdims=True), (BAND * ROWS, DIM)
        )
    over(add)
    for h in range(HEADS):
        rows = slice((h % BAND) * ROWS, (h % BAND + 1) * ROWS)
        denom = jnp.sum(total[h // BAND, rows], axis=1, keepdims=True)
        out[:, h * DIM : (h + 1) * DIM] = (accum[h // BAND, rows] / denom).astype(BF16)


def softmax(sq, keys, values, docs):
    vmem = pl.BlockSpec(memory_space=pltpu.VMEM)
    bands = HEADS // BAND
    return pl.pallas_call(
        softmax_kernel,
        out_shape=jax.ShapeDtypeStruct((ROWS, WIDTH), BF16),
        in_specs=[pl.BlockSpec(memory_space=pl.ANY), vmem, vmem, pl.BlockSpec(memory_space=pltpu.SMEM)],
        out_specs=vmem,
        scratch_shapes=[
            pltpu.VMEM((bands, BAND * ROWS, DIM), BF16),
            pltpu.VMEM((bands, BAND * ROWS, DIM), F32),
            pltpu.VMEM((bands, BAND * ROWS, DIM), F32),
            pltpu.VMEM((bands, BAND * ROWS, DIM), F32),
            pltpu.SemaphoreType.DMA((HEADS,)),
        ],
        compiler_params=pltpu.CompilerParams(vmem_limit_bytes=40 << 20),
        name="softmax",
    )(sq, keys, values, docs)


def join_kernel(lin, soft, out, mine, sems):
    p = lax.axis_index("pipe")
    peer = (1 - p, lax.axis_index("ctx"), lax.axis_index("tp"))
    barrier = pltpu.get_barrier_semaphore()
    pl.semaphore_signal(barrier, inc=1, device_id=peer, device_id_type=MESH)
    mine[...] = jnp.where(p == 0, soft[...], lin[...])
    columns = pl.ds(pl.multiple_of(p * WIDTH, WIDTH), WIDTH)
    pl.semaphore_wait(barrier, 1)
    copy = pltpu.make_async_remote_copy(
        src_ref=mine, dst_ref=out.at[0, :, columns], send_sem=sems.at[0], recv_sem=sems.at[1],
        device_id=peer, device_id_type=MESH,
    )
    copy.start()
    out[0, :, columns] = jnp.where(p == 0, lin[...], soft[...])
    copy.wait()


def join(lin, soft):
    vmem = pl.BlockSpec(memory_space=pltpu.VMEM)
    return pl.pallas_call(
        join_kernel,
        out_shape=jax.ShapeDtypeStruct((1, ROWS, 2 * WIDTH), BF16),
        in_specs=[vmem, vmem],
        out_specs=vmem,
        scratch_shapes=[pltpu.VMEM((ROWS, WIDTH), BF16), pltpu.SemaphoreType.DMA((2,))],
        compiler_params=pltpu.CompilerParams(collective_id=1, has_side_effects=True),
        name="join",
    )(lin, soft)


def local(lq, lk, lv, ld, og, gain, vp, sq, sk, docs):
    lin, keys, values = section(lq, lk, lv, ld, og, gain.reshape(1, -1), vp, sk, docs)
    soft = softmax(sq, keys.reshape(-1, DIM), values.reshape(-1, DIM), docs)
    return join(lin, soft)


def solution(mesh):
    return jax.shard_map(
        local,
        mesh=mesh,
        in_specs=(
            P("ctx", "tp"), P("ctx", "tp"), P("ctx", "tp"), P("tp", "ctx"), P("ctx", "tp"),
            P("tp"), P("tp", None, None), P("ctx", "tp"), P("ctx", "tp"), P(),
        ),
        out_specs=P("pipe", "ctx", "tp"),
        check_vma=False,
    )
```

time: 879 us -> 147 us (0.17)
  waiting for transfers between devices: 426 us -> 0 us
  blocking collectives: 193 us -> 0 us
  Pallas kernels: 0 us -> 134 us
  other arithmetic: 130 us -> 0 us
  matrix products: 66.8 us -> 0 us
  local copies, waits for them, and re-layouts: 35.5 us -> 11.7 us
  between operations: 15.3 us -> 0.05 us
    all_gather x3 -> x0, waiting for transfers between devices: 410 us -> none  [the longest x1 331 us: entering(): gathered = jax.tree.map(lambda a: lax.all_gather(a, axis), part)]
    unnamed x1 -> x0, blocking collectives: 190 us -> none
    pallas_call x0 -> x3, Pallas kernels: none -> 134 us  [the longest x1 97.1 us: section(): pl.pallas_call(section_kernel, out_shape=(jax.ShapeDtypeStruct((ROWS, WID...]
    add x97 -> x0, other arithmetic: 98.7 us -> none  [the longest x60 87.2 us: chain_combine(): later[0][:, None, None] * earlier[1] + later[1]]
    dot_general x23 -> x0, matrix products: 66.8 us -> none  [the longest x9 30.6 us: update(): jnp.einsum('gcts,sgd->gctd', probs.astype(jnp.bfloat16), value_block, pre...]
    reduce_sum x20 -> x0, other arithmetic: 24.4 us -> none  [the longest x9 23.5 us: update(): total = total * factor + jnp.sum(probs, axis=-1)]
    reshape x3 -> x0, local copies, waits for them, and re-layouts: 16 us -> none  [the longest x1 7.69 us: softmax_section(): key_blocks = key_rows.reshape(block_count, block, group_count, HEAD_DIM)]
    ppermute x1 -> x0, waiting for transfers between devices: 15.8 us -> none  [shifted(): return lax.ppermute(shard, axis, pairs)]
  transfers between devices with their start and end apart: 4 -> 0, of which waited for: 3 -> 0; matrix products, arithmetic and copies ran while one was open for 13% -> 0% of each run, Pallas kernels for 0% -> 0%
where the time goes in v1:
time: 147 us; the launch traced here: 146 us
  Pallas kernels  134 us (91%)
  local copies, waits for them, and re-layouts  11.7 us (8%)
    pallas_call x1, Pallas kernels, section(): pl.pallas_call(section_kernel, out_shape=(jax.ShapeDtypeStruct((ROWS, WID...  97.1 us
    pallas_call x1, Pallas kernels, softmax(): pl.pallas_call(softmax_kernel, out_shape=jax.ShapeDtypeStruct((ROWS, WIDT...  26 us
    unnamed x25, local copies, waits for them, and re-layouts  11.7 us
    pallas_call x1, Pallas kernels, join(): pl.pallas_call(join_kernel, out_shape=jax.ShapeDtypeStruct((1, ROWS, 2 *...  11.2 us

profile of v1, /device:TPU:230, one launch (start us, length us, event | category | flops | bytes accessed | tf_op | source)
XLA Modules:
  0.0 146.0 jit_solution(3982073113533919832)
XLA Ops:
  0.0 0.0 copy-start.1
  0.0 0.0 copy-start.2
  0.0 1.1 copy-done.2
  1.1 0.0 copy-start.3
  1.1 1.1 copy-done.3
  2.2 0.0 copy-start.4
  2.2 1.1 copy-done.4
  3.3 0.0 copy-start.5
  3.3 1.1 copy-done.5
  4.3 0.0 copy-start.6
  4.3 1.0 copy-done.6
  5.4 0.9 copy-done.8
  6.3 0.7 copy-done.9
  7.0 0.7 copy-done.10
  7.7 0.7 copy-done.11
  8.3 97.1 %section.1 = (bf16[144,1024]{1,0:T(8,128)(2,1)S(1)}, bf16[4,4,4,144,128]{4,3,2,1,0:T(8,128)(2,1)S(1)}, bf16[4,4,4,144,128]{4,3,2,1,0:T(8,128)(2,1)S(1)}) custom-call(bf16[144,2048]{1,0:T(8,128)(2,1)S(1)} %copy-done.2, bf16[144,2048]{1,0:T(8,128)(2,1)S(1)} %copy-done.3, bf16[144,2048]{1,0:T(8,128)(2,1)S(1)} %copy-done.4, f32[16,144]{1,0:T(8,128)S(1)} %copy-done.9, ...), custom_call_target="tpu_custom_call" | custom-call | tf_op jit(solution)/shard_map/section/pallas_call | solution.py:289
  105.5 0.0 copy-start.7
  105.5 0.7 copy-done.7
  106.2 0.0 copy-done.1
  106.2 26.0 %softmax.1.soft = bf16[144,1024]{1,0:T(8,128)(2,1)S(1)} custom-call(bf16[144,2048]{1,0:T(8,128)(2,1)S(1)} %copy-done.1, bf16[9216,128]{1,0:T(8,128)(2,1)S(1)} %bitcast.3, bf16[9216,128]{1,0:T(8,128)(2,1)S(1)} %bitcast.4, s32[8]{0:T(128)S(1)} %copy-done.11), custom_call_target="tpu_custom_call" | custom-call | tf_op jit(solution)/shard_map/softmax/pallas_call | solution.py:415
  132.2 0.0 copy-start
  132.2 0.7 copy-done
  132.9 11.2 %join.1 = bf16[1,144,2048]{2,1,0:T(8,128)(2,1)} custom-call(bf16[144,1024]{1,0:T(8,128)(2,1)} %copy-done.7, bf16[144,1024]{1,0:T(8,128)(2,1)} %copy-done), custom_call_target="tpu_custom_call" | custom-call | tf_op jit(solution)/shard_map/join/pallas_call | solution.py:451
  144.1 1.9 %copy.12 = bf16[1,144,2048]{2,1,0:T(8,128)(2,1)} copy(bf16[1,144,2048]{2,1,0:T(8,128)(2,1)} %join.1) | data formatting | bytes 1179648
  (4 shorter events, 0.0 us)
Async XLA Ops:
  0.0 106.2 %copy-start.1 = (bf16[144,2048]{1,0:T(8,128)(2,1)S(1)}, bf16[144,2048]{1,0:T(8,128)(2,1)}, u32[]{:S(2)}) copy-start(bf16[144,2048]{1,0:T(8,128)(2,1)} %sq.1) | copy-start | bytes 1769476
  0.0 1.1 copy-start.2
  1.1 1.1 copy-start.3
  2.2 1.1 copy-start.4
  3.3 1.1 copy-start.5
  4.3 1.0 copy-start.6
  5.4 0.9 copy-start.8
  6.3 0.7 copy-start.9
  7.0 0.7 copy-start.10
  7.7 0.7 copy-start.11
  105.5 0.7 copy-start.7
  132.2 0.7 copy-start

commit v2 on v1

v2 whole, which is shorter than its diff:
```python
import math

import jax
import jax.numpy as jnp
from jax import lax
from jax.experimental import pallas as pl
from jax.experimental.pallas import tpu as pltpu
from jax.sharding import PartitionSpec as P

MESH = pl.DeviceIdType.MESH
ALL_HEADS = 32
DIM = 128
ROWS = 144
HEADS = 8
WIDTH = HEADS * DIM
PLANE = 16
SLICE = 64
SPAN = 8 * ROWS
GROUPS = 8
PAIRS = HEADS // 2
FAR = -(2.0**100)
SLOPE = math.log2(math.e) / math.sqrt(DIM)
DOCS = 8
EPSILON = 1e-06
F32 = jnp.float32
BF16 = jnp.bfloat16


def place():
    ctx = lax.axis_index("ctx")
    return (
        lax.axis_index("pipe"),
        lax.div(ctx, 16),
        lax.rem(lax.div(ctx, 4), 4),
        lax.rem(ctx, 4),
        lax.axis_index("tp"),
    )


def doc_starts(docs, positions):
    end = jnp.int32(0)
    start = jnp.zeros_like(positions)
    for i in range(DOCS):
        end = end + docs[i]
        start = jnp.where(end <= positions, end, start)
    return start


def halves(x):
    high = x.astype(BF16)
    return high, (x - high.astype(F32)).astype(BF16)


def thirds(x):
    high = x.astype(BF16)
    rest = x - high.astype(F32)
    mid = rest.astype(BF16)
    return high, mid, (rest - mid.astype(F32)).astype(BF16)


def matmul(a, b, ca, cb):
    return lax.dot_general(a, b, (((ca,), (cb,)), ((), ())), preferred_element_type=F32)


def section_kernel(
    lq, lk, lv, ld, og, gain, vp, sq, sk, docs,
    out,
    qb, kb, vb, ldb, ogb, gb, vpb, qs, kall, vall, tags,
    bst, pbuf, ppre, pfac, zsend, zbuf, psend, yin,
    loc, sqb, linb, softb, probs, mtab, ltab,
    load_sem, qload_sem, ksend, krecv, vsend, vrecv, ssend, srecv, zs, zr, rsend, rrecv, qsend, qrecv, osend, orecv,
):
    p, z, x, y, t = place()
    spot = x * 4 + y
    ctx = z * PLANE + spot
    first = ctx * ROWS

    columns = pl.ds(pl.multiple_of(p * WIDTH, WIDTH), WIDTH)
    loads = [
        pltpu.make_async_copy(src, dst, load_sem.at[i])
        for i, (src, dst) in enumerate((
            (sk.at[:, pl.ds(pl.multiple_of(p * DIM, DIM), DIM)], kall.at[z, x, y]),
            (ld.at[pl.ds(pl.multiple_of(p * HEADS, HEADS), HEADS)], ldb),
            (lk.at[:, columns], kb),
            (lv.at[:, columns], vb),
            (lq.at[:, columns], qb),
            (og.at[:, columns], ogb),
            (gain.at[:, columns], gb),
            (vp.at[p], vpb),
        ))
    ]
    loads += [
        pltpu.make_async_copy(
            sq.at[:, pl.ds(pl.multiple_of(p * WIDTH + h * DIM, DIM), DIM)], qs.at[h], qload_sem.at[h]
        )
        for h in range(HEADS)
    ]
    for load in loads:
        load.start()

    def plane_peer(d):
        return (p, z * PLANE + lax.rem(spot + d, PLANE), t)

    def y_peer(d):
        return (p, z * PLANE + x * 4 + lax.rem(y + d, 4), t)

    def x_peer(d):
        return (p, z * PLANE + lax.rem(x + d, 4) * 4 + y, t)

    def z_peer(d):
        return (p, lax.rem(z + d, 4) * PLANE + spot, t)

    quad = [(1 - p, ctx, t), (p, ctx, 1 - t), (1 - p, ctx, 1 - t)]

    barrier = pltpu.get_barrier_semaphore()
    for peer in [plane_peer(d) for d in range(1, PLANE)] + [z_peer(d) for d in (1, 2, 3)] + quad:
        pl.semaphore_signal(barrier, inc=1, device_id=peer, device_id_type=MESH)

    row = lax.broadcasted_iota(jnp.int32, (ROWS, ROWS), 0)
    col = lax.broadcasted_iota(jnp.int32, (ROWS, ROWS), 1)
    position = first + lax.broadcasted_iota(jnp.int32, (ROWS, 1), 0)
    begin = doc_starts(docs, position) - first
    last_begin = doc_starts(docs, jnp.full((1, 1), first + ROWS - 1, jnp.int32)) - first
    lower = (row >= col).astype(F32).astype(BF16)
    same_doc = (row >= col) & (col >= begin)
    continues = (begin < 0).astype(F32)
    last_continues = (last_begin < 0).astype(F32)
    in_last = (lax.broadcasted_iota(jnp.int32, (ROWS, 1), 0) >= last_begin).astype(F32)

    loads[0].wait()
    pl.semaphore_wait(barrier, PLANE - 1 + 6)

    def remote(src, dst, send, recv, i, peer):
        return pltpu.make_async_remote_copy(
            src_ref=src, dst_ref=dst, send_sem=send.at[i], recv_sem=recv.at[i],
            device_id=peer, device_id_type=MESH,
        )

    started = []

    def start(copies):
        for copy in copies:
            copy.start()
        started.extend(copies)
        return copies

    def arrived(copies):
        for copy in copies:
            copy.wait_recv()

    near, far = pl.ds(0, 2), pl.ds(2, 2)

    def gather_1(buf, send, recv):
        mine = buf.at[z, x, y]
        return start([remote(mine, mine, send, recv, d - 1, z_peer(d)) for d in (1, 2, 3)])

    def gather_2(buf, send, recv):
        a, b = buf.at[near, x, y], buf.at[far, x, y]
        return start(
            [remote(a, a, send, recv, d + 2, x_peer(d)) for d in (1, 2, 3)]
            + [remote(b, b, send, recv, d + 5, y_peer(d)) for d in (1, 2, 3)]
        )

    def gather_3(buf, send, recv):
        a, b = buf.at[near, :, y], buf.at[far, x]
        return start(
            [remote(a, a, send, recv, d + 8, y_peer(d)) for d in (1, 2, 3)]
            + [remote(b, b, send, recv, d + 11, x_peer(d)) for d in (1, 2, 3)]
        )

    phase_k = gather_1(kall, ksend, krecv)

    loads[1].wait()
    pieces = thirds(ldb[...])
    cum_row = sum(matmul(a, lower, 1, 1) for a in pieces)
    cum_col = sum(matmul(lower, a, 1, 1) for a in pieces)

    loads[2].wait()
    loads[3].wait()
    for h in range(HEADS):
        cols = slice(h * DIM, (h + 1) * DIM)
        last = cum_row[h : h + 1, ROWS - 1 : ROWS]
        tail = jnp.exp(last - cum_col[:, h : h + 1]) * in_last
        parts = halves(vb[:, cols].astype(F32) * tail)
        state = matmul(kb[:, cols], jnp.concatenate(parts, axis=1), 0, 0)
        state = state[:, :DIM] + state[:, DIM:]
        factor = jnp.broadcast_to(jnp.exp(last) * last_continues, (8, DIM))
        for i in range(2):
            bst[2 * h + i, 0:SLICE] = state[i * SLICE : (i + 1) * SLICE]
            bst[2 * h + i, SLICE : SLICE + 8] = factor

    phase = start([
        remote(bst.at[lax.rem(spot + d, PLANE)], pbuf.at[spot], ssend, srecv, d - 1, plane_peer(d))
        for d in range(1, PLANE)
    ])
    pbuf[spot] = bst[spot]

    arrived(phase_k)
    phase_k = gather_2(kall, ksend, krecv)

    loads[4].wait()
    for h in range(HEADS):
        cols = slice(h * DIM, (h + 1) * DIM)
        scores = matmul(qb[:, cols], kb[:, cols], 1, 1)
        gap = jnp.minimum(cum_col[:, h : h + 1] - cum_row[h : h + 1, :], 0.0)
        weights = (scores * jnp.where(same_doc, jnp.exp(gap), 0.0)).astype(BF16)
        loc[:, cols] = matmul(weights, vb[:, cols], 1, 0)

    arrived(phase)
    prefix = jnp.zeros((SLICE, DIM), F32)
    factor = jnp.ones((8, DIM), F32)
    for k in range(PLANE):
        ppre[k] = prefix
        pfac[k] = factor
        f = pbuf[k, SLICE : SLICE + 8]
        prefix = prefix * f[0:1] + pbuf[k, 0:SLICE]
        factor = factor * f
    zsend[0:SLICE] = prefix
    zsend[SLICE : SLICE + 8] = factor
    phase = start([remote(zsend, zbuf.at[z], zs, zr, d - 1, z_peer(d)) for d in (1, 2, 3)])
    zbuf[z] = zsend[...]

    arrived(phase_k)
    phase_k = gather_3(kall, ksend, krecv)

    lane = lax.broadcasted_iota(jnp.int32, (1, DIM), 1)
    low = jnp.full((1, DIM), 2 * ALL_HEADS * SPAN, jnp.int32)
    high = jnp.zeros((1, DIM), jnp.int32)
    end = jnp.int32(0)
    for i in range(DOCS):
        low = jnp.where(lane == i, end, low)
        end = end + docs[i]
        high = jnp.where(lane == i, end, high)

    @pl.loop(0, 4 * PLANE)
    def _(block):
        at = block * ROWS + lax.broadcasted_iota(jnp.int32, (ROWS, 1), 0)
        tags[block] = ((at >= low) & (at < high)).astype(F32).astype(BF16)

    other = jnp.where((position >= low) & (position < high) | (lane >= DOCS), 0.0, FAR).astype(BF16)
    for h in range(HEADS):
        mtab[h] = jnp.full((ROWS, DIM), FAR, F32)
        ltab[h] = jnp.zeros((ROWS, DIM), F32)

    arrived(phase)
    state = jnp.zeros((SLICE, DIM), F32)
    for k in range(3):
        state = jnp.where(k < z, state * zbuf[k, SLICE : SLICE + 1] + zbuf[k, 0:SLICE], state)
    for k in range(PLANE):
        psend[k] = state * pfac[k, 0:1] + ppre[k]
    phase = start([
        remote(psend.at[lax.rem(spot + d, PLANE)], yin.at[spot], rsend, rrecv, d - 1, plane_peer(d))
        for d in range(1, PLANE)
    ])
    yin[spot] = psend[spot]
    for load in loads[5:]:
        load.wait()
    arrived(phase)

    squares = jnp.zeros((ROWS, DIM), F32)
    for h in range(HEADS):
        cols = slice(h * DIM, (h + 1) * DIM)
        parts = halves(yin[2 * h : 2 * h + 2].reshape(DIM, DIM))
        carried = matmul(qb[:, cols], jnp.concatenate(parts, axis=1), 1, 0)
        weight = jnp.exp(cum_col[:, h : h + 1]) * continues
        attention = loc[:, cols] + weight * (carried[:, :DIM] + carried[:, DIM:])
        loc[:, cols] = attention
        squares = squares + attention * attention

    eye = row == col
    total = jnp.sum(squares, axis=1, keepdims=True)
    sqb[0] = jnp.broadcast_to(jnp.sum(jnp.where(eye, total, 0.0), axis=0, keepdims=True), (8, ROWS))
    phase = start([
        remote(sqb.at[0], sqb.at[i + 1], qsend, qrecv, i, quad[i]) for i in range(3)
    ])
    for h in range(HEADS):
        cols = slice(h * DIM, (h + 1) * DIM)
        gate = jax.nn.sigmoid(ogb[:, cols].astype(F32))
        loc[:, cols] = loc[:, cols] * (gb[:, cols] * gate)
    arrived(phase)
    total = sqb[0, 0:1] + sqb[1, 0:1] + (sqb[2, 0:1] + sqb[3, 0:1])
    total = jnp.sum(jnp.where(eye, total, 0.0), axis=1, keepdims=True)
    scale = lax.rsqrt(total / (ALL_HEADS * DIM) + EPSILON)
    for h in range(HEADS):
        cols = slice(h * DIM, (h + 1) * DIM)
        linb[:, cols] = (loc[:, cols] * scale).astype(BF16)
    vall[z, x, y] = matmul(linb[...], vpb[...], 1, 0).astype(BF16)
    phase_v = gather_1(vall, vsend, vrecv)

    lin_copy = remote(linb, out.at[0, :, columns], osend, orecv, 0, quad[0])

    @pl.when(p == 1)
    def _():
        lin_copy.start()

    @pl.when(p == 0)
    def _():
        out[0, :, columns] = linb[...]

    arrived(phase_k)

    def probe(group, diagonal):
        over = group // 2
        wide = pl.ds(2 * lax.rem(group, 2), 2)
        keys = jnp.concatenate(
            [
                kall[over, wide].reshape(SPAN, DIM),
                tags[pl.ds(group * 8, 8)].reshape(SPAN, DIM),
            ],
            axis=1,
        )

        @pl.loop(0, PAIRS)
        def _(pair):
            for i in range(2):
                h = 2 * pair + i
                scores = matmul(jnp.concatenate([qs[h], other], axis=1), keys, 1, 1)
                if diagonal:
                    at = group * SPAN + lax.broadcasted_iota(jnp.int32, (1, SPAN), 1)
                    scores = jnp.where(at <= position, scores, FAR)
                top = jnp.max(scores, axis=1, keepdims=True)
                prob = jnp.exp2((scores - top) * SLOPE)
                denom = jnp.sum(prob, axis=1, keepdims=True)
                probs[group, h] = prob.astype(BF16)
                mtab[h] = jnp.where(lane == group, top, mtab[h])
                ltab[h] = jnp.where(lane == group, denom, ltab[h])

    whole = lax.div(ctx, 8)
    part = lax.div(whole, 3)
    probe(whole, True)
    arrived(phase_v)
    phase_v = gather_2(vall, vsend, vrecv)

    @pl.loop(jnp.int32(0), part)
    def _(group):
        probe(group, False)

    arrived(phase_v)
    phase_v = gather_3(vall, vsend, vrecv)

    @pl.loop(part, whole)
    def _(group):
        probe(group, False)

    for h in range(HEADS):
        table = mtab[h]
        top = jnp.max(table, axis=1, keepdims=True)
        share = jnp.exp2((table - top) * SLOPE)
        denom = jnp.sum(share * ltab[h], axis=1, keepdims=True)
        mtab[h] = share
        ltab[h] = jnp.broadcast_to(denom, (ROWS, DIM))
    arrived(phase_v)

    soft_copies = [
        remote(softb.at[i], out.at[0, :, pl.ds(pl.multiple_of(p * WIDTH + 2 * i * DIM, 2 * DIM), 2 * DIM)],
               osend, orecv, i + 1, quad[0])
        for i in range(PAIRS)
    ]
    for i in range(PAIRS):
        def step(group, sums):
            values = vall[group // 2, pl.ds(2 * lax.rem(group, 2), 2)].reshape(SPAN, DIM)
            result = []
            for j in range(2):
                share = jnp.sum(jnp.where(lane == group, mtab[2 * i + j], 0.0), axis=1, keepdims=True)
                result.append(sums[j] + share * matmul(probs[group, 2 * i + j], values, 1, 0))
            return tuple(result)

        sums = lax.fori_loop(
            jnp.int32(0), whole + 1, step, (jnp.zeros((ROWS, DIM), F32), jnp.zeros((ROWS, DIM), F32))
        )
        for j in range(2):
            softb[i, :, j * DIM : (j + 1) * DIM] = (sums[j] / ltab[2 * i + j]).astype(BF16)

        @pl.when(p == 0)
        def _():
            soft_copies[i].start()

        @pl.when(p == 1)
        def _():
            out[0, :, pl.ds(pl.multiple_of(p * WIDTH + 2 * i * DIM, 2 * DIM), 2 * DIM)] = softb[i]

    for copy in started:
        copy.wait_send()

    @pl.when(p == 0)
    def _():
        for copy in soft_copies:
            copy.wait_send()
        lin_copy.wait_recv()

    @pl.when(p == 1)
    def _():
        lin_copy.wait_send()
        for copy in soft_copies:
            copy.wait_recv()


def local(lq, lk, lv, ld, og, gain, vp, sq, sk, docs):
    anywhere = pl.BlockSpec(memory_space=pl.ANY)
    vmem = pl.BlockSpec(memory_space=pltpu.VMEM)
    dma = lambda n: pltpu.SemaphoreType.DMA((n,))
    blocks = (4, 4, 4, ROWS, DIM)
    return pl.pallas_call(
        section_kernel,
        out_shape=jax.ShapeDtypeStruct((1, ROWS, 2 * WIDTH), BF16),
        in_specs=[anywhere] * 9 + [pl.BlockSpec(memory_space=pltpu.SMEM)],
        out_specs=vmem,
        scratch_shapes=[
            pltpu.VMEM((ROWS, WIDTH), BF16),
            pltpu.VMEM((ROWS, WIDTH), BF16),
            pltpu.VMEM((ROWS, WIDTH), BF16),
            pltpu.VMEM((HEADS, ROWS), F32),
            pltpu.VMEM((ROWS, WIDTH), BF16),
            pltpu.VMEM((1, WIDTH), F32),
            pltpu.VMEM((WIDTH, DIM), BF16),
            pltpu.VMEM((HEADS, ROWS, DIM), BF16),
            pltpu.VMEM(blocks, BF16),
            pltpu.VMEM(blocks, BF16),
            pltpu.VMEM((4 * PLANE, ROWS, DIM), BF16),
            pltpu.VMEM((PLANE, SLICE + 8, DIM), F32),
            pltpu.VMEM((PLANE, SLICE + 8, DIM), F32),
            pltpu.VMEM((PLANE, SLICE, DIM), F32),
            pltpu.VMEM((PLANE, 8, DIM), F32),
            pltpu.VMEM((SLICE + 8, DIM), F32),
            pltpu.VMEM((4, SLICE + 8, DIM), F32),
            pltpu.VMEM((PLANE, SLICE, DIM), F32),
            pltpu.VMEM((PLANE, SLICE, DIM), F32),
            pltpu.VMEM((ROWS, WIDTH), F32),
            pltpu.VMEM((4, 8, ROWS), F32),
            pltpu.VMEM((ROWS, WIDTH), BF16),
            pltpu.VMEM((PAIRS, ROWS, 2 * DIM), BF16),
            pltpu.VMEM((GROUPS, HEADS, ROWS, SPAN), BF16),
            pltpu.VMEM((HEADS, ROWS, DIM), F32),
            pltpu.VMEM((HEADS, ROWS, DIM), F32),
            dma(8), dma(8), dma(15), dma(15), dma(15), dma(15), dma(15), dma(15), dma(3), dma(3),
            dma(15), dma(15), dma(3), dma(3), dma(5), dma(5),
        ],
        compiler_params=pltpu.CompilerParams(
            collective_id=0, has_side_effects=True, vmem_limit_bytes=60 << 20
        ),
        name="section",
    )(lq, lk, lv, ld, og, gain.reshape(1, -1), vp, sq, sk, docs)


def solution(mesh):
    return jax.shard_map(
        local,
        mesh=mesh,
        in_specs=(
            P("ctx", "tp"), P("ctx", "tp"), P("ctx", "tp"), P("tp", "ctx"), P("ctx", "tp"),
            P("tp"), P("tp", None, None), P("ctx", "tp"), P("ctx", "tp"), P(),
        ),
        out_specs=P("pipe", "ctx", "tp"),
        check_vma=False,
    )
```

time: 147 us -> 89.9 us (0.61)
  Pallas kernels: 134 us -> 87.8 us
  local copies, waits for them, and re-layouts: 11.7 us -> 1.93 us
    pallas_call x3 -> x1, Pallas kernels: 134 us -> 87.8 us  [local(): pl.pallas_call(section_kernel, out_shape=jax.ShapeDtypeStruct((1, ROWS, 2...]
    unnamed x25 -> x1, local copies, waits for them, and re-layouts: 11.7 us -> 1.93 us
where the time goes in v2:
time: 89.9 us; the launch traced here: 89.7 us
  Pallas kernels  87.8 us (98%)
  local copies, waits for them, and re-layouts  1.93 us (2%)
    pallas_call x1, Pallas kernels, local(): pl.pallas_call(section_kernel, out_shape=jax.ShapeDtypeStruct((1, ROWS, 2...  87.8 us
    unnamed x1, local copies, waits for them, and re-layouts  1.93 us

profile of v2, /device:TPU:230, one launch (start us, length us, event | category | flops | bytes accessed | tf_op | source)
XLA Modules:
  0.0 89.7 jit_solution(18036134824940687399)
XLA Ops:
  0.0 87.8 %section.1 = bf16[1,144,2048]{2,1,0:T(8,128)(2,1)} custom-call(bf16[144,2048]{1,0:T(8,128)(2,1)} %lq.1, bf16[144,2048]{1,0:T(8,128)(2,1)} %lk.1, bf16[144,2048]{1,0:T(8,128)(2,1)} %lv.1, f32[16,144]{1,0:T(8,128)} %ld.1, bf16[144,2048]{1,0:T(8,128)(2,1)} %og.1, f32[1,2048]{1,0:T(1,128)} %bitcast.1, bf16[2,1024,128]{2,1,0:T(8,128)(2,1)} %vp.1, ...), custom_call_target="tpu_custom_call" | custom-call | tf_op jit(solution)/shard_map/section/pallas_call | solution.py:403
  87.8 1.9 %copy.12 = bf16[1,144,2048]{2,1,0:T(8,128)(2,1)} copy(bf16[1,144,2048]{2,1,0:T(8,128)(2,1)} %section.1) | data formatting | bytes 1179648

commit v3 on v2

--- a/solution.py
+++ b/solution.py
@@ -17,7 +17,8 @@
 SLICE = 64
 SPAN = 8 * ROWS
 GROUPS = 8
-PAIRS = HEADS // 2
+TEAM = 4
+TEAMS = HEADS // TEAM
 FAR = -(2.0**100)
 SLOPE = math.log2(math.e) / math.sqrt(DIM)
 DOCS = 8
@@ -67,7 +68,7 @@
     out,
     qb, kb, vb, ldb, ogb, gb, vpb, qs, kall, vall, tags,
     bst, pbuf, ppre, pfac, zsend, zbuf, psend, yin,
-    loc, sqb, linb, softb, probs, mtab, ltab,
+    loc, sqb, linb, softb, probs, mtab, ltab, asum,
     load_sem, qload_sem, ksend, krecv, vsend, vrecv, ssend, srecv, zs, zr, rsend, rrecv, qsend, qrecv, osend, orecv,
 ):
     p, z, x, y, t = place()
@@ -161,11 +162,11 @@
             + [remote(b, b, send, recv, d + 5, y_peer(d)) for d in (1, 2, 3)]
         )
 
-    def gather_3(buf, send, recv):
-        a, b = buf.at[near, :, y], buf.at[far, x]
+    def gather_3(buf, send, recv, half):
+        a, b = buf.at[half, :, y], buf.at[half + 2, x]
         return start(
-            [remote(a, a, send, recv, d + 8, y_peer(d)) for d in (1, 2, 3)]
-            + [remote(b, b, send, recv, d + 11, x_peer(d)) for d in (1, 2, 3)]
+            [remote(a, a, send, recv, d + 8 + 6 * half, y_peer(d)) for d in (1, 2, 3)]
+            + [remote(b, b, send, recv, d + 11 + 6 * half, x_peer(d)) for d in (1, 2, 3)]
         )
 
     phase_k = gather_1(kall, ksend, krecv)
@@ -194,9 +195,6 @@
         for d in range(1, PLANE)
     ])
     pbuf[spot] = bst[spot]
-
-    arrived(phase_k)
-    phase_k = gather_2(kall, ksend, krecv)
 
     loads[4].wait()
     for h in range(HEADS):
@@ -221,7 +219,7 @@
     zbuf[z] = zsend[...]
 
     arrived(phase_k)
-    phase_k = gather_3(kall, ksend, krecv)
+    phase_k = gather_2(kall, ksend, krecv)
 
     lane = lax.broadcasted_iota(jnp.int32, (1, DIM), 1)
     low = jnp.full((1, DIM), 2 * ALL_HEADS * SPAN, jnp.int32)
@@ -238,6 +236,7 @@
         tags[block] = ((at >= low) & (at < high)).astype(F32).astype(BF16)
 
     other = jnp.where((position >= low) & (position < high) | (lane >= DOCS), 0.0, FAR).astype(BF16)
+    others = jnp.concatenate([other] * TEAM, axis=0)
     for h in range(HEADS):
         mtab[h] = jnp.full((ROWS, DIM), FAR, F32)
         ltab[h] = jnp.zeros((ROWS, DIM), F32)
@@ -255,7 +254,9 @@
     yin[spot] = psend[spot]
     for load in loads[5:]:
         load.wait()
+    arrived(phase_k)
     arrived(phase)
+    phase_k = [gather_3(kall, ksend, krecv, half) for half in (0, 1)]
 
     squares = jnp.zeros((ROWS, DIM), F32)
     for h in range(HEADS):
@@ -287,17 +288,9 @@
     vall[z, x, y] = matmul(linb[...], vpb[...], 1, 0).astype(BF16)
     phase_v = gather_1(vall, vsend, vrecv)
 
-    lin_copy = remote(linb, out.at[0, :, columns], osend, orecv, 0, quad[0])
-
-    @pl.when(p == 1)
-    def _():
-        lin_copy.start()
-
     @pl.when(p == 0)
     def _():
         out[0, :, columns] = linb[...]
-
-    arrived(phase_k)
 
     def probe(group, diagonal):
         over = group // 2
@@ -310,11 +303,14 @@
             axis=1,
         )
 
-        @pl.loop(0, PAIRS)
-        def _(pair):
-            for i in range(2):
-                h = 2 * pair + i
-                scores = matmul(jnp.concatenate([qs[h], other], axis=1), keys, 1, 1)
+        @pl.loop(0, TEAMS)
+        def _(team):
+            heads = pl.ds(team * TEAM, TEAM)
+            asked = jnp.concatenate([qs[heads].reshape(TEAM * ROWS, DIM), others], axis=1)
+            raw = matmul(asked, keys, 1, 1)
+            for i in range(TEAM):
+                h = team * TEAM + i
+                scores = raw[i * ROWS : (i + 1) * ROWS]
                 if diagonal:
                     at = group * SPAN + lax.broadcasted_iota(jnp.int32, (1, SPAN), 1)
                     scores = jnp.where(at <= position, scores, FAR)
@@ -326,21 +322,33 @@
                 ltab[h] = jnp.where(lane == group, denom, ltab[h])
 
     whole = lax.div(ctx, 8)
-    part = lax.div(whole, 3)
-    probe(whole, True)
+
+    def nth(half, i):
+        return lax.div(i, 2) * 4 + lax.rem(i, 2) + 2 * half
+
+    def below(half, limit):
+        return sum(lax.div(limit + 7 - nth(half, jnp.int32(i)), 8) for i in range(4))
+
+    def probe_half(half):
+        @pl.loop(jnp.int32(0), below(half, whole))
+        def _(i):
+            probe(nth(half, i), False)
+
     arrived(phase_v)
     phase_v = gather_2(vall, vsend, vrecv)
-
-    @pl.loop(jnp.int32(0), part)
-    def _(group):
-        probe(group, False)
-
+    lin_copy = remote(linb, out.at[0, :, columns], osend, orecv, 0, quad[0])
+
+    @pl.when(p == 1)
+    def _():
+        lin_copy.start()
+
+    arrived(phase_k[0])
+    probe_half(0)
     arrived(phase_v)
-    phase_v = gather_3(vall, vsend, vrecv)
-
-    @pl.loop(part, whole)
-    def _(group):
-        probe(group, False)
+    phase_v = [gather_3(vall, vsend, vrecv, half) for half in (0, 1)]
+    arrived(phase_k[1])
+    probe(whole, True)
+    probe_half(1)
 
     for h in range(HEADS):
         table = mtab[h]
@@ -349,35 +357,47 @@
         denom = jnp.sum(share * ltab[h], axis=1, keepdims=True)
         mtab[h] = share
         ltab[h] = jnp.broadcast_to(denom, (ROWS, DIM))
-    arrived(phase_v)
+
+    def gathered(half, team, sums):
+        def step(n, sums):
+            group = nth(half, n)
+            values = vall[group // 2, pl.ds(2 * lax.rem(group, 2), 2)].reshape(SPAN, DIM)
+            heads = pl.ds(team * TEAM, TEAM)
+            product = matmul(probs[group, heads].reshape(TEAM * ROWS, SPAN), values, 1, 0)
+            result = []
+            for i in range(TEAM):
+                share = jnp.sum(jnp.where(lane == group, mtab[team * TEAM + i], 0.0), axis=1, keepdims=True)
+                result.append(sums[i] + share * product[i * ROWS : (i + 1) * ROWS])
+            return tuple(result)
+
+        return lax.fori_loop(jnp.int32(0), below(half, whole + 1), step, sums)
+
+    arrived(phase_v[0])
+    for team in range(TEAMS):
+        sums = gathered(0, team, tuple(jnp.zeros((ROWS, DIM), F32) for _ in range(TEAM)))
+        for i in range(TEAM):
+            asum[team * TEAM + i] = sums[i]
+    arrived(phase_v[1])
+
+    def team_columns(team):
+        return pl.ds(pl.multiple_of(p * WIDTH + team * TEAM * DIM, TEAM * DIM), TEAM * DIM)
 
     soft_copies = [
-        remote(softb.at[i], out.at[0, :, pl.ds(pl.multiple_of(p * WIDTH + 2 * i * DIM, 2 * DIM), 2 * DIM)],
-               osend, orecv, i + 1, quad[0])
-        for i in range(PAIRS)
+        remote(softb.at[team], out.at[0, :, team_columns(team)], osend, orecv, team + 1, quad[0])
+        for team in range(TEAMS)
     ]
-    for i in range(PAIRS):
-        def step(group, sums):
-            values = vall[group // 2, pl.ds(2 * lax.rem(group, 2), 2)].reshape(SPAN, DIM)
-            result = []
-            for j in range(2):
-                share = jnp.sum(jnp.where(lane == group, mtab[2 * i + j], 0.0), axis=1, keepdims=True)
-                result.append(sums[j] + share * matmul(probs[group, 2 * i + j], values, 1, 0))
-            return tuple(result)
-
-        sums = lax.fori_loop(
-            jnp.int32(0), whole + 1, step, (jnp.zeros((ROWS, DIM), F32), jnp.zeros((ROWS, DIM), F32))
-        )
-        for j in range(2):
-            softb[i, :, j * DIM : (j + 1) * DIM] = (sums[j] / ltab[2 * i + j]).astype(BF16)
+    for team in range(TEAMS):
+        sums = gathered(1, team, tuple(asum[team * TEAM + i] for i in range(TEAM)))
+        for i in range(TEAM):
+            softb[team, :, i * DIM : (i + 1) * DIM] = (sums[i] / ltab[team * TEAM + i]).astype(BF16)
 
         @pl.when(p == 0)
         def _():
-            soft_copies[i].start()
+            soft_copies[team].start()
 
         @pl.when(p == 1)
         def _():
-            out[0, :, pl.ds(pl.multiple_of(p * WIDTH + 2 * i * DIM, 2 * DIM), 2 * DIM)] = softb[i]
+            out[0, :, team_columns(team)] = softb[team]
 
     for copy in started:
         copy.wait_send()
@@ -428,12 +448,13 @@
             pltpu.VMEM((ROWS, WIDTH), F32),
             pltpu.VMEM((4, 8, ROWS), F32),
             pltpu.VMEM((ROWS, WIDTH), BF16),
-            pltpu.VMEM((PAIRS, ROWS, 2 * DIM), BF16),
+            pltpu.VMEM((TEAMS, ROWS, TEAM * DIM), BF16),
             pltpu.VMEM((GROUPS, HEADS, ROWS, SPAN), BF16),
             pltpu.VMEM((HEADS, ROWS, DIM), F32),
             pltpu.VMEM((HEADS, ROWS, DIM), F32),
-            dma(8), dma(8), dma(15), dma(15), dma(15), dma(15), dma(15), dma(15), dma(3), dma(3),
-            dma(15), dma(15), dma(3), dma(3), dma(5), dma(5),
+            pltpu.VMEM((HEADS, ROWS, DIM), F32),
+            dma(8), dma(8), dma(21), dma(21), dma(21), dma(21), dma(15), dma(15), dma(3), dma(3),
+            dma(15), dma(15), dma(3), dma(3), dma(1 + TEAMS), dma(1 + TEAMS),
         ],
         compiler_params=pltpu.CompilerParams(
             collective_id=0, has_side_effects=True, vmem_limit_bytes=60 << 20

time: 89.9 us -> 78.2 us (0.87); the launches traced: 89.7 us -> 76.9 us
  Pallas kernels: 87.8 us -> 74.9 us
    pallas_call x1, Pallas kernels: 87.8 us -> 74.9 us  [local(): pl.pallas_call(section_kernel, out_shape=jax.ShapeDtypeStruct((1, ROWS, 2...]
where the time goes in v3:
time: 78.2 us; the launch traced here: 76.9 us
  Pallas kernels  74.9 us (96%)
  local copies, waits for them, and re-layouts  1.93 us (2%)
    pallas_call x1, Pallas kernels, local(): pl.pallas_call(section_kernel, out_shape=jax.ShapeDtypeStruct((1, ROWS, 2...  74.9 us
    unnamed x1, local copies, waits for them, and re-layouts  1.93 us

profile of v3, /device:TPU:230, one launch (start us, length us, event | category | flops | bytes accessed | tf_op | source)
XLA Modules:
  0.0 76.9 jit_solution(3781709389042237054)
XLA Ops:
  0.0 74.9 %section.1 = bf16[1,144,2048]{2,1,0:T(8,128)(2,1)} custom-call(bf16[144,2048]{1,0:T(8,128)(2,1)} %lq.1, bf16[144,2048]{1,0:T(8,128)(2,1)} %lk.1, bf16[144,2048]{1,0:T(8,128)(2,1)} %lv.1, f32[16,144]{1,0:T(8,128)} %ld.1, bf16[144,2048]{1,0:T(8,128)(2,1)} %og.1, f32[1,2048]{1,0:T(1,128)} %bitcast.1, bf16[2,1024,128]{2,1,0:T(8,128)(2,1)} %vp.1, ...), custom_call_target="tpu_custom_call" | custom-call | tf_op jit(solution)/shard_map/section/pallas_call | solution.py:423
  74.9 1.9 %copy.12 = bf16[1,144,2048]{2,1,0:T(8,128)(2,1)} copy(bf16[1,144,2048]{2,1,0:T(8,128)(2,1)} %section.1) | data formatting | bytes 1179648

commit v4 on v3

--- a/solution.py
+++ b/solution.py
@@ -19,6 +19,7 @@
 GROUPS = 8
 TEAM = 4
 TEAMS = HEADS // TEAM
+PARTS = ((0, 4), (4, 4))
 FAR = -(2.0**100)
 SLOPE = math.log2(math.e) / math.sqrt(DIM)
 DOCS = 8
@@ -69,7 +70,7 @@
     qb, kb, vb, ldb, ogb, gb, vpb, qs, kall, vall, tags,
     bst, pbuf, ppre, pfac, zsend, zbuf, psend, yin,
     loc, sqb, linb, softb, probs, mtab, ltab, asum,
-    load_sem, qload_sem, ksend, krecv, vsend, vrecv, ssend, srecv, zs, zr, rsend, rrecv, qsend, qrecv, osend, orecv,
+    load_sem, qload_sem, ksend, krecv, vsend, vrecv, ssend, srecv, zs, zr, rsend, rrecv, qsend, qrecv, osend, orecv, own_sem,
 ):
     p, z, x, y, t = place()
     spot = x * 4 + y
@@ -96,8 +97,6 @@
         )
         for h in range(HEADS)
     ]
-    for load in loads:
-        load.start()
 
     def plane_peer(d):
         return (p, z * PLANE + lax.rem(spot + d, PLANE), t)
@@ -116,6 +115,8 @@
     barrier = pltpu.get_barrier_semaphore()
     for peer in [plane_peer(d) for d in range(1, PLANE)] + [z_peer(d) for d in (1, 2, 3)] + quad:
         pl.semaphore_signal(barrier, inc=1, device_id=peer, device_id_type=MESH)
+    for load in loads:
+        load.start()
 
     row = lax.broadcasted_iota(jnp.int32, (ROWS, ROWS), 0)
     col = lax.broadcasted_iota(jnp.int32, (ROWS, ROWS), 1)
@@ -139,35 +140,53 @@
 
     started = []
 
+    def only(condition, act, copies):
+        def all_of_them():
+            for copy in copies:
+                act(copy)
+
+        if condition is None:
+            all_of_them()
+        else:
+            pl.when(condition)(all_of_them)
+
+    def start_bundles(bundles):
+        for copies, sends, _ in bundles:
+            only(sends, lambda copy: copy.start(), copies)
+        started.extend(bundles)
+        return bundles
+
     def start(copies):
-        for copy in copies:
-            copy.start()
-        started.extend(copies)
-        return copies
-
-    def arrived(copies):
-        for copy in copies:
-            copy.wait_recv()
-
-    near, far = pl.ds(0, 2), pl.ds(2, 2)
+        return start_bundles([(copies, None, None)])
+
+    def arrived(bundles):
+        for copies, _, receives in bundles:
+            only(receives, lambda copy: copy.wait_recv(), copies)
+
+    def upto(layer):
+        return None if layer == 0 else z >= layer
 
     def gather_1(buf, send, recv):
         mine = buf.at[z, x, y]
-        return start([remote(mine, mine, send, recv, d - 1, z_peer(d)) for d in (1, 2, 3)])
+        return start_bundles([
+            ([remote(mine, mine, send, recv, d - 1, z_peer(d))], z + d < 4, z >= d) for d in (1, 2, 3)
+        ])
 
     def gather_2(buf, send, recv):
-        a, b = buf.at[near, x, y], buf.at[far, x, y]
-        return start(
-            [remote(a, a, send, recv, d + 2, x_peer(d)) for d in (1, 2, 3)]
-            + [remote(b, b, send, recv, d + 5, y_peer(d)) for d in (1, 2, 3)]
-        )
+        bundles = []
+        for layer in range(4):
+            mine, peer = buf.at[layer, x, y], x_peer if layer < 2 else y_peer
+            copies = [remote(mine, mine, send, recv, 3 * layer + d + 2, peer(d)) for d in (1, 2, 3)]
+            bundles.append((copies, upto(layer), upto(layer)))
+        return start_bundles(bundles)
 
     def gather_3(buf, send, recv, half):
         a, b = buf.at[half, :, y], buf.at[half + 2, x]
-        return start(
-            [remote(a, a, send, recv, d + 8 + 6 * half, y_peer(d)) for d in (1, 2, 3)]
-            + [remote(b, b, send, recv, d + 11 + 6 * half, x_peer(d)) for d in (1, 2, 3)]
-        )
+        via_y = [remote(a, a, send, recv, d + 14 + 6 * half, y_peer(d)) for d in (1, 2, 3)]
+        via_x = [remote(b, b, send, recv, d + 17 + 6 * half, x_peer(d)) for d in (1, 2, 3)]
+        return start_bundles([
+            (via_y, upto(half), upto(half)), (via_x, upto(half + 2), upto(half + 2)),
+        ])
 
     phase_k = gather_1(kall, ksend, krecv)
 
@@ -236,7 +255,7 @@
         tags[block] = ((at >= low) & (at < high)).astype(F32).astype(BF16)
 
     other = jnp.where((position >= low) & (position < high) | (lane >= DOCS), 0.0, FAR).astype(BF16)
-    others = jnp.concatenate([other] * TEAM, axis=0)
+    others = jnp.concatenate([other] * HEADS, axis=0)
     for h in range(HEADS):
         mtab[h] = jnp.full((ROWS, DIM), FAR, F32)
         ltab[h] = jnp.zeros((ROWS, DIM), F32)
@@ -288,9 +307,11 @@
     vall[z, x, y] = matmul(linb[...], vpb[...], 1, 0).astype(BF16)
     phase_v = gather_1(vall, vsend, vrecv)
 
+    lin_own = pltpu.make_async_copy(linb, out.at[0, :, columns], own_sem.at[len(PARTS)])
+
     @pl.when(p == 0)
     def _():
-        out[0, :, columns] = linb[...]
+        lin_own.start()
 
     def probe(group, diagonal):
         over = group // 2
@@ -303,13 +324,11 @@
             axis=1,
         )
 
-        @pl.loop(0, TEAMS)
-        def _(team):
-            heads = pl.ds(team * TEAM, TEAM)
-            asked = jnp.concatenate([qs[heads].reshape(TEAM * ROWS, DIM), others], axis=1)
+        if True:
+            asked = jnp.concatenate([qs[...].reshape(HEADS * ROWS, DIM), others], axis=1)
             raw = matmul(asked, keys, 1, 1)
-            for i in range(TEAM):
-                h = team * TEAM + i
+            for h in range(HEADS):
+                i = h
                 scores = raw[i * ROWS : (i + 1) * ROWS]
                 if diagonal:
                     at = group * SPAN + lax.broadcasted_iota(jnp.int32, (1, SPAN), 1)
@@ -329,8 +348,8 @@
     def below(half, limit):
         return sum(lax.div(limit + 7 - nth(half, jnp.int32(i)), 8) for i in range(4))
 
-    def probe_half(half):
-        @pl.loop(jnp.int32(0), below(half, whole))
+    def probe_half(half, low, high):
+        @pl.loop(low, high)
         def _(i):
             probe(nth(half, i), False)
 
@@ -343,12 +362,14 @@
         lin_copy.start()
 
     arrived(phase_k[0])
-    probe_half(0)
+    ready, some = below(0, whole), lax.div(below(0, whole), 2)
+    probe_half(0, jnp.int32(0), some)
     arrived(phase_v)
     phase_v = [gather_3(vall, vsend, vrecv, half) for half in (0, 1)]
+    probe_half(0, some, ready)
     arrived(phase_k[1])
     probe(whole, True)
-    probe_half(1)
+    probe_half(1, jnp.int32(0), below(1, whole))
 
     for h in range(HEADS):
         table = mtab[h]
@@ -358,38 +379,42 @@
         mtab[h] = share
         ltab[h] = jnp.broadcast_to(denom, (ROWS, DIM))
 
-    def gathered(half, team, sums):
+    def gathered(half, start_head, size, sums):
         def step(n, sums):
             group = nth(half, n)
             values = vall[group // 2, pl.ds(2 * lax.rem(group, 2), 2)].reshape(SPAN, DIM)
-            heads = pl.ds(team * TEAM, TEAM)
-            product = matmul(probs[group, heads].reshape(TEAM * ROWS, SPAN), values, 1, 0)
+            heads = pl.ds(start_head, size)
+            product = matmul(probs[group, heads].reshape(size * ROWS, SPAN), values, 1, 0)
             result = []
-            for i in range(TEAM):
-                share = jnp.sum(jnp.where(lane == group, mtab[team * TEAM + i], 0.0), axis=1, keepdims=True)
+            for i in range(size):
+                share = jnp.sum(jnp.where(lane == group, mtab[start_head + i], 0.0), axis=1, keepdims=True)
                 result.append(sums[i] + share * product[i * ROWS : (i + 1) * ROWS])
             return tuple(result)
 
         return lax.fori_loop(jnp.int32(0), below(half, whole + 1), step, sums)
 
     arrived(phase_v[0])
-    for team in range(TEAMS):
-        sums = gathered(0, team, tuple(jnp.zeros((ROWS, DIM), F32) for _ in range(TEAM)))
-        for i in range(TEAM):
-            asum[team * TEAM + i] = sums[i]
+    sums = gathered(0, 0, HEADS, tuple(jnp.zeros((ROWS, DIM), F32) for _ in range(HEADS)))
+    for h in range(HEADS):
+        asum[h] = sums[h]
     arrived(phase_v[1])
 
-    def team_columns(team):
-        return pl.ds(pl.multiple_of(p * WIDTH + team * TEAM * DIM, TEAM * DIM), TEAM * DIM)
+    def share_of(part):
+        low, size = PARTS[part]
+        return softb.at[:, pl.ds(low * DIM, size * DIM)], out.at[
+            0, :, pl.ds(pl.multiple_of(p * WIDTH + low * DIM, 2 * DIM), size * DIM)
+        ]
 
     soft_copies = [
-        remote(softb.at[team], out.at[0, :, team_columns(team)], osend, orecv, team + 1, quad[0])
-        for team in range(TEAMS)
+        remote(*share_of(part), osend, orecv, part + 1, quad[0]) for part in range(len(PARTS))
     ]
-    for team in range(TEAMS):
-        sums = gathered(1, team, tuple(asum[team * TEAM + i] for i in range(TEAM)))
-        for i in range(TEAM):
-            softb[team, :, i * DIM : (i + 1) * DIM] = (sums[i] / ltab[team * TEAM + i]).astype(BF16)
+    soft_own = [
+        pltpu.make_async_copy(*share_of(part), own_sem.at[part]) for part in range(len(PARTS))
+    ]
+    for team, (low, size) in enumerate(PARTS):
+        sums = gathered(1, low, size, tuple(asum[low + i] for i in range(size)))
+        for i in range(size):
+            softb[:, (low + i) * DIM : (low + i + 1) * DIM] = (sums[i] / ltab[low + i]).astype(BF16)
 
         @pl.when(p == 0)
         def _():
@@ -397,20 +422,23 @@
 
         @pl.when(p == 1)
         def _():
-            out[0, :, team_columns(team)] = softb[team]
-
-    for copy in started:
-        copy.wait_send()
+            soft_own[team].start()
+
+    for copies, sends, _ in started:
+        only(sends, lambda copy: copy.wait_send(), copies)
 
     @pl.when(p == 0)
     def _():
         for copy in soft_copies:
             copy.wait_send()
         lin_copy.wait_recv()
+        lin_own.wait()
 
     @pl.when(p == 1)
     def _():
         lin_copy.wait_send()
+        for copy in soft_own:
+            copy.wait()
         for copy in soft_copies:
             copy.wait_recv()
 
@@ -424,7 +452,7 @@
         section_kernel,
         out_shape=jax.ShapeDtypeStruct((1, ROWS, 2 * WIDTH), BF16),
         in_specs=[anywhere] * 9 + [pl.BlockSpec(memory_space=pltpu.SMEM)],
-        out_specs=vmem,
+        out_specs=anywhere,
         scratch_shapes=[
             pltpu.VMEM((ROWS, WIDTH), BF16),
             pltpu.VMEM((ROWS, WIDTH), BF16),
@@ -448,13 +476,13 @@
             pltpu.VMEM((ROWS, WIDTH), F32),
             pltpu.VMEM((4, 8, ROWS), F32),
             pltpu.VMEM((ROWS, WIDTH), BF16),
-            pltpu.VMEM((TEAMS, ROWS, TEAM * DIM), BF16),
+            pltpu.VMEM((ROWS, WIDTH), BF16),
             pltpu.VMEM((GROUPS, HEADS, ROWS, SPAN), BF16),
             pltpu.VMEM((HEADS, ROWS, DIM), F32),
             pltpu.VMEM((HEADS, ROWS, DIM), F32),
             pltpu.VMEM((HEADS, ROWS, DIM), F32),
-            dma(8), dma(8), dma(21), dma(21), dma(21), dma(21), dma(15), dma(15), dma(3), dma(3),
-            dma(15), dma(15), dma(3), dma(3), dma(1 + TEAMS), dma(1 + TEAMS),
+            dma(8), dma(8), dma(27), dma(27), dma(27), dma(27), dma(15), dma(15), dma(3), dma(3),
+            dma(15), dma(15), dma(3), dma(3), dma(1 + len(PARTS)), dma(1 + len(PARTS)), dma(1 + len(PARTS)),
         ],
         compiler_params=pltpu.CompilerParams(
             collective_id=0, has_side_effects=True, vmem_limit_bytes=60 << 20

time: 78.2 us -> 75.2 us (0.962)
  Pallas kernels: 74.9 us -> 72.2 us
    pallas_call x1, Pallas kernels: 74.9 us -> 72.2 us  [local(): pl.pallas_call(section_kernel, out_shape=jax.ShapeDtypeStruct((1, ROWS, 2...]
where the time goes in v4:
time: 75.2 us; the launch traced here: 74.2 us
  Pallas kernels  72.2 us (96%)
  local copies, waits for them, and re-layouts  1.93 us (3%)
    pallas_call x1, Pallas kernels, local(): pl.pallas_call(section_kernel, out_shape=jax.ShapeDtypeStruct((1, ROWS, 2...  72.2 us
    unnamed x1, local copies, waits for them, and re-layouts  1.93 us

profile of v4, /device:TPU:230, one launch (start us, length us, event | category | flops | bytes accessed | tf_op | source)
XLA Modules:
  0.0 74.2 jit_solution(5335880384194969149)
XLA Ops:
  0.0 72.2 %section.1 = bf16[1,144,2048]{2,1,0:T(8,128)(2,1)} custom-call(bf16[144,2048]{1,0:T(8,128)(2,1)} %lq.1, bf16[144,2048]{1,0:T(8,128)(2,1)} %lk.1, bf16[144,2048]{1,0:T(8,128)(2,1)} %lv.1, f32[16,144]{1,0:T(8,128)} %ld.1, bf16[144,2048]{1,0:T(8,128)(2,1)} %og.1, f32[1,2048]{1,0:T(1,128)} %bitcast.1, bf16[2,1024,128]{2,1,0:T(8,128)(2,1)} %vp.1, ...), custom_call_target="tpu_custom_call" | custom-call | tf_op jit(solution)/shard_map/section/pallas_call | solution.py:451
  72.2 1.9 %copy.12 = bf16[1,144,2048]{2,1,0:T(8,128)(2,1)} copy(bf16[1,144,2048]{2,1,0:T(8,128)(2,1)} %section.1) | data formatting | bytes 1179648

commit v5 on v4

--- a/solution.py
+++ b/solution.py
@@ -69,7 +69,7 @@
     out,
     qb, kb, vb, ldb, ogb, gb, vpb, qs, kall, vall, tags,
     bst, pbuf, ppre, pfac, zsend, zbuf, psend, yin,
-    loc, sqb, linb, softb, probs, mtab, ltab, asum,
+    loc, sqb, linb, softb, probs, mtab, ltab, dsum, asum,
     load_sem, qload_sem, ksend, krecv, vsend, vrecv, ssend, srecv, zs, zr, rsend, rrecv, qsend, qrecv, osend, orecv, own_sem,
 ):
     p, z, x, y, t = place()
@@ -258,7 +258,7 @@
     others = jnp.concatenate([other] * HEADS, axis=0)
     for h in range(HEADS):
         mtab[h] = jnp.full((ROWS, DIM), FAR, F32)
-        ltab[h] = jnp.zeros((ROWS, DIM), F32)
+        dsum[h] = jnp.zeros((ROWS, DIM), F32)
 
     arrived(phase)
     state = jnp.zeros((SLICE, DIM), F32)
@@ -335,10 +335,9 @@
                     scores = jnp.where(at <= position, scores, FAR)
                 top = jnp.max(scores, axis=1, keepdims=True)
                 prob = jnp.exp2((scores - top) * SLOPE)
-                denom = jnp.sum(prob, axis=1, keepdims=True)
                 probs[group, h] = prob.astype(BF16)
                 mtab[h] = jnp.where(lane == group, top, mtab[h])
-                ltab[h] = jnp.where(lane == group, denom, ltab[h])
+                ltab[group, h] = sum(prob[:, k : k + DIM] for k in range(0, SPAN, DIM))
 
     whole = lax.div(ctx, 8)
 
@@ -374,10 +373,7 @@
     for h in range(HEADS):
         table = mtab[h]
         top = jnp.max(table, axis=1, keepdims=True)
-        share = jnp.exp2((table - top) * SLOPE)
-        denom = jnp.sum(share * ltab[h], axis=1, keepdims=True)
-        mtab[h] = share
-        ltab[h] = jnp.broadcast_to(denom, (ROWS, DIM))
+        mtab[h] = jnp.exp2((table - top) * SLOPE)
 
     def gathered(half, start_head, size, sums):
         def step(n, sums):
@@ -388,6 +384,7 @@
             result = []
             for i in range(size):
                 share = jnp.sum(jnp.where(lane == group, mtab[start_head + i], 0.0), axis=1, keepdims=True)
+                dsum[start_head + i] += share * ltab[group, start_head + i]
                 result.append(sums[i] + share * product[i * ROWS : (i + 1) * ROWS])
             return tuple(result)
 
@@ -414,7 +411,9 @@
     for team, (low, size) in enumerate(PARTS):
         sums = gathered(1, low, size, tuple(asum[low + i] for i in range(size)))
         for i in range(size):
-            softb[:, (low + i) * DIM : (low + i + 1) * DIM] = (sums[i] / ltab[low + i]).astype(BF16)
+            softb[:, (low + i) * DIM : (low + i + 1) * DIM] = (
+                sums[i] / jnp.sum(dsum[low + i], axis=1, keepdims=True)
+            ).astype(BF16)
 
         @pl.when(p == 0)
         def _():
@@ -479,6 +478,7 @@
             pltpu.VMEM((ROWS, WIDTH), BF16),
             pltpu.VMEM((GROUPS, HEADS, ROWS, SPAN), BF16),
             pltpu.VMEM((HEADS, ROWS, DIM), F32),
+            pltpu.VMEM((GROUPS, HEADS, ROWS, DIM), F32),
             pltpu.VMEM((HEADS, ROWS, DIM), F32),
             pltpu.VMEM((HEADS, ROWS, DIM), F32),
             dma(8), dma(8), dma(27), dma(27), dma(27), dma(27), dma(15), dma(15), dma(3), dma(3),

time: 75.2 us -> 74.3 us (0.988)
  Pallas kernels: 72.2 us -> 71.3 us
    pallas_call x1, Pallas kernels: 72.2 us -> 71.3 us  [local(): pl.pallas_call(section_kernel, out_shape=jax.ShapeDtypeStruct((1, ROWS, 2...]
where the time goes in v5:
time: 74.3 us; the launch traced here: 73.2 us
  Pallas kernels  71.3 us (96%)
  local copies, waits for them, and re-layouts  1.93 us (3%)
    pallas_call x1, Pallas kernels, local(): pl.pallas_call(section_kernel, out_shape=jax.ShapeDtypeStruct((1, ROWS, 2...  71.3 us
    unnamed x1, local copies, waits for them, and re-layouts  1.93 us

profile of v5, /device:TPU:230, one launch (start us, length us, event | category | flops | bytes accessed | tf_op | source)
XLA Modules:
  0.0 73.2 jit_solution(2571310587492486979)
XLA Ops:
  0.0 71.3 %section.1 = bf16[1,144,2048]{2,1,0:T(8,128)(2,1)} custom-call(bf16[144,2048]{1,0:T(8,128)(2,1)} %lq.1, bf16[144,2048]{1,0:T(8,128)(2,1)} %lk.1, bf16[144,2048]{1,0:T(8,128)(2,1)} %lv.1, f32[16,144]{1,0:T(8,128)} %ld.1, bf16[144,2048]{1,0:T(8,128)(2,1)} %og.1, f32[1,2048]{1,0:T(1,128)} %bitcast.1, bf16[2,1024,128]{2,1,0:T(8,128)(2,1)} %vp.1, ...), custom_call_target="tpu_custom_call" | custom-call | tf_op jit(solution)/shard_map/section/pallas_call | solution.py:450
  71.3 1.9 %copy.12 = bf16[1,144,2048]{2,1,0:T(8,128)(2,1)} copy(bf16[1,144,2048]{2,1,0:T(8,128)(2,1)} %section.1) | data formatting | bytes 1179648

commit v6 on v5

--- a/solution.py
+++ b/solution.py
@@ -19,7 +19,7 @@
 GROUPS = 8
 TEAM = 4
 TEAMS = HEADS // TEAM
-PARTS = ((0, 4), (4, 4))
+PARTS = ((0, 2), (2, 2), (4, 2), (6, 2))
 FAR = -(2.0**100)
 SLOPE = math.log2(math.e) / math.sqrt(DIM)
 DOCS = 8

time: 74.3 us -> 74.3 us (level)
  no operation moved by 1% of the time
where the time goes in v6:
time: 74.3 us; the launch traced here: 73.1 us
  Pallas kernels  71.2 us (96%)
  local copies, waits for them, and re-layouts  1.93 us (3%)
    pallas_call x1, Pallas kernels, local(): pl.pallas_call(section_kernel, out_shape=jax.ShapeDtypeStruct((1, ROWS, 2...  71.2 us
    unnamed x1, local copies, waits for them, and re-layouts  1.93 us

profile of v6, /device:TPU:230, one launch (start us, length us, event | category | flops | bytes accessed | tf_op | source)
XLA Modules:
  0.0 73.1 jit_solution(1199992047845251736)
XLA Ops:
  0.0 71.2 %section.1 = bf16[1,144,2048]{2,1,0:T(8,128)(2,1)} custom-call(bf16[144,2048]{1,0:T(8,128)(2,1)} %lq.1, bf16[144,2048]{1,0:T(8,128)(2,1)} %lk.1, bf16[144,2048]{1,0:T(8,128)(2,1)} %lv.1, f32[16,144]{1,0:T(8,128)} %ld.1, bf16[144,2048]{1,0:T(8,128)(2,1)} %og.1, f32[1,2048]{1,0:T(1,128)} %bitcast.1, bf16[2,1024,128]{2,1,0:T(8,128)(2,1)} %vp.1, ...), custom_call_target="tpu_custom_call" | custom-call | tf_op jit(solution)/shard_map/section/pallas_call | solution.py:450
  71.2 1.9 %copy.12 = bf16[1,144,2048]{2,1,0:T(8,128)(2,1)} copy(bf16[1,144,2048]{2,1,0:T(8,128)(2,1)} %section.1) | data formatting | bytes 1179648
